TPU v7x, 32 devices: a whole 2x2x4 slice. The times are simulated.
32 devices in a mesh: groups: 2 (over x), win: 4 (over z), lat: 4 (over y, core).
Axes of the slice: x: 2, y: 2, z: 4, core: 2. Of those that a mesh axis runs over, the one named last changes fastest.
Arguments:
- thickness: float32 [8, 2, 3, 8, 64, 256], P(('groups', 'win'), None, None, None, 'lat'), parts along dimension 0, may hold values from 0.5 to 1.5
- obs_cells: int32 [8, 2, 1024], P(('groups', 'win'), None, 'lat'), parts along dimension 0, may hold values from 0 to 4095
- obs_values: float32 [8, 2, 1024], P(('groups', 'win'), None, 'lat'), parts along dimension 0, may hold values from -6 to 6
- ocean_mask: int32 [128, 256], P(('groups', 'lat')), parts along dimension 0, may hold values 0 or 1
- coupling: float32 [8, 8], replicated, may hold values from -1.2 to 1.2
- damping: float32 [8], replicated, may hold values from 0.05 to 0.8
Outputs:
- window_adjoint: float32 [8, 3, 8, 64, 256], P(('groups', 'win'), None, None, 'lat'), parts along dimension 0
- bias_gradient: float32 [16, 64, 256], P('groups', 'lat'), parts along dimension 0
There are 2 independent parts, one for each index of `groups`. A program takes and returns all parts, laid end to end along the dimension named above; an argument that names none is the same for every part. Nothing has to cross between parts.
Inputs may be any that keep to these rules, and one draw needn't show every extreme that they name: `obs_cells`: entry k of a step's list names a cell of the latitude block that starts at row (k // 256) * 16, as row * 256 + column within that block; a cell may be named several times.
All inputs are finite; a program needn't handle non-finite values. No bound on the sum of `ocean_mask` on one device may be relied on, other than what follows from the above.
Results may differ from a plain program's by a relative error of at most 0.00011.
Values sent between devices are 32-bit elements; how exact they have to be, the bound alone decides.
No kernel may reach another device: no remote copies, remote signals or barrier semaphores. Data moves between devices by JAX's collectives and lax.ppermute only.
A program may use at most 64 MiB of HBM per device.

v0:
```python
import jax
import jax.numpy as jnp
from jax import lax
from jax.sharding import PartitionSpec as P

STEP_DT = 0.2
THIRD = 1.0 / 3.0
TWO_THIRDS = 2.0 / 3.0


def with_halo(value, sides, width):
    for axis, dim in sides:
        count, length = (lax.axis_size(axis), value.shape[dim])
        up = [(i, (i + 1) % count) for i in range(count - 1)]
        down = [(j, i) for i, j in up]
        last = lax.slice_in_dim(value, length - width, length, axis=dim)
        initial = lax.slice_in_dim(value, 0, width, axis=dim)
        before = lax.ppermute(last, axis, up)
        after = lax.ppermute(initial, axis, down)
        value = jnp.concatenate([before, value, after], axis=dim)
    return value


def passed_along(value, axis, steps):
    count = lax.axis_size(axis)
    initial, last = (max(0, -steps), min(count, count - steps))
    return lax.ppermute(value, axis, [(source, source + steps) for source in range(initial, last)])


def tendency(state, ocean, fcor, edges, mix, rate):
    p_part = state[1]
    q_part = state[2]
    a_part = state[0]
    w_mid = edges[0][:, 1:-1]
    dxp = 0.5 * (jnp.roll(p_part, -1, axis=2) - jnp.roll(p_part, 1, axis=2))
    dyq = 0.5 * (edges[1][:, 2:] - edges[1][:, :-2])
    mixed = jnp.einsum("kl,krc->lrc", mix, dxp + dyq, precision=lax.Precision.HIGHEST)
    t_a = ocean * (mixed - rate * a_part)
    t_p = ocean * (
        0.5 * (jnp.roll(w_mid, -1, axis=2) - jnp.roll(w_mid, 1, axis=2))
        + fcor * q_part
        - rate * p_part
    )
    t_q = ocean * (0.5 * (edges[0][:, 2:] - edges[0][:, :-2]) - fcor * p_part - rate * q_part)
    return jnp.stack([t_a, t_p, t_q])


def runge_kutta(state, section_tend):
    first = state + STEP_DT * section_tend(state, 0)
    second = 0.75 * state + 0.25 * (first + STEP_DT * section_tend(first, 1))
    return THIRD * state + TWO_THIRDS * (second + STEP_DT * section_tend(second, 2))


def add_obs(state, cells, values):
    layer_a = state[0]
    flat = layer_a.reshape(layer_a.shape[0], -1).at[:, cells].add(values[None, :])
    return state.at[0].set(flat.reshape(layer_a.shape))


def per_device(thickness, obs_cells, obs_values, ocean_mask, coupling, damping):
    rows = ocean_mask.shape[0]
    total_rows = rows * lax.axis_size("lat")
    first_row = lax.axis_index("lat") * rows
    mix = jnp.eye(coupling.shape[0], dtype=jnp.float32) + coupling
    rate = damping[:, None, None]
    steps = thickness.shape[1]
    ocean = ocean_mask.astype(jnp.float32)
    global_rows = first_row + jnp.arange(rows, dtype=jnp.int32)
    fcor = (0.3 + 0.4 * (global_rows.astype(jnp.float32) / total_rows - 0.5))[:, None]

    def adjoint_step(state, thick):

        def section_tend(current, section):
            pair = jnp.stack([thick[section] * current[0], current[2]])
            edges = with_halo(pair, (("lat", 2),), 1)
            return tendency(current, ocean, fcor, edges, mix, rate)

        return runge_kutta(state, section_tend)

    def integrate(state):
        bias = jnp.zeros(state.shape[1:], jnp.float32)
        for step in reversed(range(steps)):
            state = add_obs(state, obs_cells[0, step], obs_values[0, step])
            state = adjoint_step(state, thickness[0, step])
            bias = bias + STEP_DT * state[0]
        return (state, bias)

    zero_state = jnp.zeros((3,) + thickness.shape[3:], jnp.float32)
    rounds = lax.axis_size("win") - 1

    def relay_round(index, carry):
        start_state, unused = integrate(carry)
        return passed_along(start_state, "win", -1)

    incoming = lax.fori_loop(0, rounds, relay_round, zero_state)
    lam, bias = integrate(incoming)
    total_bias = lax.psum(bias, "win")
    return (lam[None], total_bias)


def solution(mesh):
    in_specs = (
        P(("groups", "win"), None, None, None, "lat", None),
        P(("groups", "win"), None, "lat"),
        P(("groups", "win"), None, "lat"),
        P(("groups", "lat"), None),
        P(),
        P(),
    )
    out_specs = (P(("groups", "win"), None, None, "lat", None), P("groups", "lat", None))
    return jax.shard_map(
        per_device, mesh=mesh, in_specs=in_specs, out_specs=out_specs, check_vma=False
    )
```

profile of v0, /device:TPU:0, one launch (start us, length us, event | category | flops | bytes accessed | tf_op | source)
XLA Modules:
  0.0 356.3 jit_solution(15236490072825664713)
XLA Ops:
  7.9 1.6 copy.105
  10.9 1.3 compare_select_fusion.2
  12.2 1.4 fusion.377
  13.6 232.1 %while.17 = (s32[]{:T(128)}, f32[3,8,16,256]{3,1,2,0:T(8,128)S(1)}, s32[1,2,256]{2,1,0:T(2,128)}, f32[1,2,256]{2,1,0:T(2,128)}, f32[16,256]{1,0:T(8,128)S(1)}, /...) while((s32[]{:T(128)}, f32[3,8,16,256]{3,1,2,0:T(8,128)S(1)}, ...), condition=%wide.region_3.4_spmd.clone, body=%wide.region_0.3_spmd.clone.sunk | while | flops 31856224 | bytes 54825772 | solution.py:95
  14.9 1.4 fusion.444
  16.9 2.8 scatter_custom_fusion.16
  22.2 3.6 %collective-permute-start.1 = (f32[2,8,1,256]{3,1,2,0:T(8,128)}, f32[2,8,1,256]{3,1,2,0:T(8,128)}, u32[]{:S(2)}, u32[]{:S(2)}) collective-permute-start(f32[2,8,1,256]{3,1,2,0:T(8,128)} %get-tuple-element.585), channel_id=1, source_target_pairs={{0,1},{1,2},{2,3},{4,5},{5,6},{6,7},{8,9},{9,10},{10,11},{12,13},{... | collective-permute-start | bytes 49160 | tf_op jit(solution)/shard_map/while/body/eval_jaxpr/ppermute | solution.py:18
  30.1 1.3 collective-permute-start.2
  31.4 4.5 %collective-permute-start.3 = (f32[2,8,1,256]{3,1,2,0:T(8,128)S(1)}, f32[2,8,1,256]{3,1,2,0:T(8,128)S(1)}, u32[]{:S(2)}, u32[]{:S(2)}) collective-permute-start(f32[2,8,1,256]{3,1,2,0:T(8,128)S(1)} %get-tuple-element.601), channel_id=1, source_target_pairs={{0,1},{1,2},{2,3},{4,5},{5,6},{6,7},{8,9},{9,10},{10,11},{12,13},{... | collective-permute-start | bytes 49160 | tf_op jit(solution)/shard_map/while/body/eval_jaxpr/ppermute | solution.py:18
  38.5 1.3 collective-permute-start.4
  39.8 4.3 %collective-permute-start.5 = (f32[2,8,1,256]{3,1,2,0:T(8,128)S(1)}, f32[2,8,1,256]{3,1,2,0:T(8,128)S(1)}, u32[]{:S(2)}, u32[]{:S(2)}) collective-permute-start(f32[2,8,1,256]{3,1,2,0:T(8,128)S(1)} %get-tuple-element.617), channel_id=1, source_target_pairs={{0,1},{1,2},{2,3},{4,5},{5,6},{6,7},{8,9},{9,10},{10,11},{12,13},{... | collective-permute-start | bytes 49160 | tf_op jit(solution)/shard_map/while/body/eval_jaxpr/ppermute | solution.py:18
  47.3 2.9 scatter_custom_fusion.17
  51.8 1.3 collective-permute-start.6
  53.1 4.9 %collective-permute-start.7 = (f32[2,8,1,256]{3,1,2,0:T(8,128)S(1)}, f32[2,8,1,256]{3,1,2,0:T(8,128)S(1)}, u32[]{:S(2)}, u32[]{:S(2)}) collective-permute-start(f32[2,8,1,256]{3,1,2,0:T(8,128)S(1)} %get-tuple-element.635), channel_id=1, source_target_pairs={{0,1},{1,2},{2,3},{4,5},{5,6},{6,7},{8,9},{9,10},{10,11},{12,13},{... | collective-permute-start | bytes 49160 | tf_op jit(solution)/shard_map/while/body/eval_jaxpr/ppermute | solution.py:18
  60.7 1.3 collective-permute-start.8
  62.0 4.9 %collective-permute-start.9 = (f32[2,8,1,256]{3,1,2,0:T(8,128)S(1)}, f32[2,8,1,256]{3,1,2,0:T(8,128)S(1)}, u32[]{:S(2)}, u32[]{:S(2)}) collective-permute-start(f32[2,8,1,256]{3,1,2,0:T(8,128)S(1)} %get-tuple-element.651), channel_id=1, source_target_pairs={{0,1},{1,2},{2,3},{4,5},{5,6},{6,7},{8,9},{9,10},{10,11},{12,13},{... | collective-permute-start | bytes 49160 | tf_op jit(solution)/shard_map/while/body/eval_jaxpr/ppermute | solution.py:18
  69.5 1.3 collective-permute-start.10
  70.8 4.9 %collective-permute-start.11 = (f32[2,8,1,256]{3,1,2,0:T(8,128)S(1)}, f32[2,8,1,256]{3,1,2,0:T(8,128)S(1)}, u32[]{:S(2)}, u32[]{:S(2)}) collective-permute-start(f32[2,8,1,256]{3,1,2,0:T(8,128)S(1)} %get-tuple-element.667), channel_id=1, source_target_pairs={{0,1},{1,2},{2,3},{4,5},{5,6},{6,7},{8,9},{9,10},{10,11},{12,13},{... | collective-permute-start | bytes 49160 | tf_op jit(solution)/shard_map/while/body/eval_jaxpr/ppermute | solution.py:18
  78.2 1.3 collective-permute-start.12
  79.5 11.2 %collective-permute-done.12 = f32[3,8,16,256]{3,1,2,0:T(8,128)S(1)} collective-permute-done((f32[3,8,16,256]{3,1,2,0:T(8,128)S(1)}, f32[3,8,16,256]{3,1,2,0:T(8,128)S(1)}, u32[]{:S(2)}, u32[]{:S(2)}) %collective-permute-start.12) | collective-permute-done | bytes 393248 | tf_op jit(solution)/shard_map/while/body/eval_jaxpr/ppermute | solution.py:27
  92.0 1.4 fusion.444
  93.9 2.8 scatter_custom_fusion.16
  99.2 4.4 %collective-permute-start.1 = (f32[2,8,1,256]{3,1,2,0:T(8,128)}, f32[2,8,1,256]{3,1,2,0:T(8,128)}, u32[]{:S(2)}, u32[]{:S(2)}) collective-permute-start(f32[2,8,1,256]{3,1,2,0:T(8,128)} %get-tuple-element.585), channel_id=1, source_target_pairs={{0,1},{1,2},{2,3},{4,5},{5,6},{6,7},{8,9},{9,10},{10,11},{12,13},{... | collective-permute-start | bytes 49160 | tf_op jit(solution)/shard_map/while/body/eval_jaxpr/ppermute | solution.py:18
  107.8 1.3 collective-permute-start.2
  109.1 4.3 %collective-permute-start.3 = (f32[2,8,1,256]{3,1,2,0:T(8,128)S(1)}, f32[2,8,1,256]{3,1,2,0:T(8,128)S(1)}, u32[]{:S(2)}, u32[]{:S(2)}) collective-permute-start(f32[2,8,1,256]{3,1,2,0:T(8,128)S(1)} %get-tuple-element.601), channel_id=1, source_target_pairs={{0,1},{1,2},{2,3},{4,5},{5,6},{6,7},{8,9},{9,10},{10,11},{12,13},{... | collective-permute-start | bytes 49160 | tf_op jit(solution)/shard_map/while/body/eval_jaxpr/ppermute | solution.py:18
  116.0 1.3 collective-permute-start.4
  117.3 4.3 %collective-permute-start.5 = (f32[2,8,1,256]{3,1,2,0:T(8,128)S(1)}, f32[2,8,1,256]{3,1,2,0:T(8,128)S(1)}, u32[]{:S(2)}, u32[]{:S(2)}) collective-permute-start(f32[2,8,1,256]{3,1,2,0:T(8,128)S(1)} %get-tuple-element.617), channel_id=1, source_target_pairs={{0,1},{1,2},{2,3},{4,5},{5,6},{6,7},{8,9},{9,10},{10,11},{12,13},{... | collective-permute-start | bytes 49160 | tf_op jit(solution)/shard_map/while/body/eval_jaxpr/ppermute | solution.py:18
  124.8 2.9 scatter_custom_fusion.17
  129.3 1.3 collective-permute-start.6
  130.6 4.9 %collective-permute-start.7 = (f32[2,8,1,256]{3,1,2,0:T(8,128)S(1)}, f32[2,8,1,256]{3,1,2,0:T(8,128)S(1)}, u32[]{:S(2)}, u32[]{:S(2)}) collective-permute-start(f32[2,8,1,256]{3,1,2,0:T(8,128)S(1)} %get-tuple-element.635), channel_id=1, source_target_pairs={{0,1},{1,2},{2,3},{4,5},{5,6},{6,7},{8,9},{9,10},{10,11},{12,13},{... | collective-permute-start | bytes 49160 | tf_op jit(solution)/shard_map/while/body/eval_jaxpr/ppermute | solution.py:18
  138.3 1.3 collective-permute-start.8
  139.6 4.9 %collective-permute-start.9 = (f32[2,8,1,256]{3,1,2,0:T(8,128)S(1)}, f32[2,8,1,256]{3,1,2,0:T(8,128)S(1)}, u32[]{:S(2)}, u32[]{:S(2)}) collective-permute-start(f32[2,8,1,256]{3,1,2,0:T(8,128)S(1)} %get-tuple-element.651), channel_id=1, source_target_pairs={{0,1},{1,2},{2,3},{4,5},{5,6},{6,7},{8,9},{9,10},{10,11},{12,13},{... | collective-permute-start | bytes 49160 | tf_op jit(solution)/shard_map/while/body/eval_jaxpr/ppermute | solution.py:18
  147.0 1.3 collective-permute-start.10
  148.3 4.9 %collective-permute-start.11 = (f32[2,8,1,256]{3,1,2,0:T(8,128)S(1)}, f32[2,8,1,256]{3,1,2,0:T(8,128)S(1)}, u32[]{:S(2)}, u32[]{:S(2)}) collective-permute-start(f32[2,8,1,256]{3,1,2,0:T(8,128)S(1)} %get-tuple-element.667), channel_id=1, source_target_pairs={{0,1},{1,2},{2,3},{4,5},{5,6},{6,7},{8,9},{9,10},{10,11},{12,13},{... | collective-permute-start | bytes 49160 | tf_op jit(solution)/shard_map/while/body/eval_jaxpr/ppermute | solution.py:18
  155.7 1.3 collective-permute-start.12
  157.0 11.2 %collective-permute-done.12 = f32[3,8,16,256]{3,1,2,0:T(8,128)S(1)} collective-permute-done((f32[3,8,16,256]{3,1,2,0:T(8,128)S(1)}, f32[3,8,16,256]{3,1,2,0:T(8,128)S(1)}, u32[]{:S(2)}, u32[]{:S(2)}) %collective-permute-start.12) | collective-permute-done | bytes 393248 | tf_op jit(solution)/shard_map/while/body/eval_jaxpr/ppermute | solution.py:27
  169.5 1.4 fusion.444
  171.4 2.8 scatter_custom_fusion.16
  176.7 4.4 %collective-permute-start.1 = (f32[2,8,1,256]{3,1,2,0:T(8,128)}, f32[2,8,1,256]{3,1,2,0:T(8,128)}, u32[]{:S(2)}, u32[]{:S(2)}) collective-permute-start(f32[2,8,1,256]{3,1,2,0:T(8,128)} %get-tuple-element.585), channel_id=1, source_target_pairs={{0,1},{1,2},{2,3},{4,5},{5,6},{6,7},{8,9},{9,10},{10,11},{12,13},{... | collective-permute-start | bytes 49160 | tf_op jit(solution)/shard_map/while/body/eval_jaxpr/ppermute | solution.py:18
  185.4 1.3 collective-permute-start.2
  186.7 4.3 %collective-permute-start.3 = (f32[2,8,1,256]{3,1,2,0:T(8,128)S(1)}, f32[2,8,1,256]{3,1,2,0:T(8,128)S(1)}, u32[]{:S(2)}, u32[]{:S(2)}) collective-permute-start(f32[2,8,1,256]{3,1,2,0:T(8,128)S(1)} %get-tuple-element.601), channel_id=1, source_target_pairs={{0,1},{1,2},{2,3},{4,5},{5,6},{6,7},{8,9},{9,10},{10,11},{12,13},{... | collective-permute-start | bytes 49160 | tf_op jit(solution)/shard_map/while/body/eval_jaxpr/ppermute | solution.py:18
  193.5 1.3 collective-permute-start.4
  194.8 4.3 %collective-permute-start.5 = (f32[2,8,1,256]{3,1,2,0:T(8,128)S(1)}, f32[2,8,1,256]{3,1,2,0:T(8,128)S(1)}, u32[]{:S(2)}, u32[]{:S(2)}) collective-permute-start(f32[2,8,1,256]{3,1,2,0:T(8,128)S(1)} %get-tuple-element.617), channel_id=1, source_target_pairs={{0,1},{1,2},{2,3},{4,5},{5,6},{6,7},{8,9},{9,10},{10,11},{12,13},{... | collective-permute-start | bytes 49160 | tf_op jit(solution)/shard_map/while/body/eval_jaxpr/ppermute | solution.py:18
  202.3 2.9 scatter_custom_fusion.17
  206.8 1.3 collective-permute-start.6
  208.1 4.9 %collective-permute-start.7 = (f32[2,8,1,256]{3,1,2,0:T(8,128)S(1)}, f32[2,8,1,256]{3,1,2,0:T(8,128)S(1)}, u32[]{:S(2)}, u32[]{:S(2)}) collective-permute-start(f32[2,8,1,256]{3,1,2,0:T(8,128)S(1)} %get-tuple-element.635), channel_id=1, source_target_pairs={{0,1},{1,2},{2,3},{4,5},{5,6},{6,7},{8,9},{9,10},{10,11},{12,13},{... | collective-permute-start | bytes 49160 | tf_op jit(solution)/shard_map/while/body/eval_jaxpr/ppermute | solution.py:18
  217.1 4.9 %collective-permute-start.9 = (f32[2,8,1,256]{3,1,2,0:T(8,128)S(1)}, f32[2,8,1,256]{3,1,2,0:T(8,128)S(1)}, u32[]{:S(2)}, u32[]{:S(2)}) collective-permute-start(f32[2,8,1,256]{3,1,2,0:T(8,128)S(1)} %get-tuple-element.651), channel_id=1, source_target_pairs={{0,1},{1,2},{2,3},{4,5},{5,6},{6,7},{8,9},{9,10},{10,11},{12,13},{... | collective-permute-start | bytes 49160 | tf_op jit(solution)/shard_map/while/body/eval_jaxpr/ppermute | solution.py:18
  225.8 4.9 %collective-permute-start.11 = (f32[2,8,1,256]{3,1,2,0:T(8,128)S(1)}, f32[2,8,1,256]{3,1,2,0:T(8,128)S(1)}, u32[]{:S(2)}, u32[]{:S(2)}) collective-permute-start(f32[2,8,1,256]{3,1,2,0:T(8,128)S(1)} %get-tuple-element.667), channel_id=1, source_target_pairs={{0,1},{1,2},{2,3},{4,5},{5,6},{6,7},{8,9},{9,10},{10,11},{12,13},{... | collective-permute-start | bytes 49160 | tf_op jit(solution)/shard_map/while/body/eval_jaxpr/ppermute | solution.py:18
  234.5 11.2 %collective-permute-done.12 = f32[3,8,16,256]{3,1,2,0:T(8,128)S(1)} collective-permute-done((f32[3,8,16,256]{3,1,2,0:T(8,128)S(1)}, f32[3,8,16,256]{3,1,2,0:T(8,128)S(1)}, u32[]{:S(2)}, u32[]{:S(2)}) %collective-permute-start.12) | collective-permute-done | bytes 393248 | tf_op jit(solution)/shard_map/while/body/eval_jaxpr/ppermute | solution.py:27
  246.4 3.1 scatter_custom_fusion.2
  250.1 3.1 collective-permute-start.13
  255.8 2.4 collective-permute-done.14
  260.8 4.4 %collective-permute-start.15 = (f32[2,8,1,256]{3,1,2,0:T(8,128)S(1)}, f32[2,8,1,256]{3,1,2,0:T(8,128)S(1)}, u32[]{:S(2)}, u32[]{:S(2)}) collective-permute-start(f32[2,8,1,256]{3,1,2,0:T(8,128)S(1)} %get-tuple-element.365), channel_id=1, source_target_pairs={{0,1},{1,2},{2,3},{4,5},{5,6},{6,7},{8,9},{9,10},{10,11},{12,13},{... | collective-permute-start | bytes 49160 | tf_op jit(solution)/shard_map/ppermute | solution.py:18
  266.5 1.8 collective-permute-done.16
  270.0 3.9 %collective-permute-start.17 = (f32[2,8,1,256]{3,1,2,0:T(8,128)S(1)}, f32[2,8,1,256]{3,1,2,0:T(8,128)S(1)}, u32[]{:S(2)}, u32[]{:S(2)}) collective-permute-start(f32[2,8,1,256]{3,1,2,0:T(8,128)S(1)} %get-tuple-element.363), channel_id=1, source_target_pairs={{0,1},{1,2},{2,3},{4,5},{5,6},{6,7},{8,9},{9,10},{10,11},{12,13},{... | collective-permute-start | bytes 49160 | tf_op jit(solution)/shard_map/ppermute | solution.py:18
  275.2 1.8 collective-permute-done.18
  280.1 2.9 scatter_custom_fusion.3
  284.3 3.9 %collective-permute-start.19 = (f32[2,8,1,256]{3,1,2,0:T(8,128)S(1)}, f32[2,8,1,256]{3,1,2,0:T(8,128)S(1)}, u32[]{:S(2)}, u32[]{:S(2)}) collective-permute-start(f32[2,8,1,256]{3,1,2,0:T(8,128)S(1)} %get-tuple-element.361), channel_id=1, source_target_pairs={{0,1},{1,2},{2,3},{4,5},{5,6},{6,7},{8,9},{9,10},{10,11},{12,13},{... | collective-permute-start | bytes 49160 | tf_op jit(solution)/shard_map/ppermute | solution.py:18
  293.9 3.9 %collective-permute-start.21 = (f32[2,8,1,256]{3,1,2,0:T(8,128)S(1)}, f32[2,8,1,256]{3,1,2,0:T(8,128)S(1)}, u32[]{:S(2)}, u32[]{:S(2)}) collective-permute-start(f32[2,8,1,256]{3,1,2,0:T(8,128)S(1)} %get-tuple-element.359), channel_id=1, source_target_pairs={{0,1},{1,2},{2,3},{4,5},{5,6},{6,7},{8,9},{9,10},{10,11},{12,13},{... | collective-permute-start | bytes 49160 | tf_op jit(solution)/shard_map/ppermute | solution.py:18
  299.1 1.8 collective-permute-done.22
  302.6 3.9 %collective-permute-start.23 = (f32[2,8,1,256]{3,1,2,0:T(8,128)S(1)}, f32[2,8,1,256]{3,1,2,0:T(8,128)S(1)}, u32[]{:S(2)}, u32[]{:S(2)}) collective-permute-start(f32[2,8,1,256]{3,1,2,0:T(8,128)S(1)} %get-tuple-element.357), channel_id=1, source_target_pairs={{0,1},{1,2},{2,3},{4,5},{5,6},{6,7},{8,9},{9,10},{10,11},{12,13},{... | collective-permute-start | bytes 49160 | tf_op jit(solution)/shard_map/ppermute | solution.py:18
  307.9 1.8 collective-permute-done.24
  313.3 34.5 %all-reduce.2.cloned.1.call-done = f32[8,16,256]{2,0,1:T(8,128)} async-done(((f32[8,16,256]{2,0,1:T(8,128)}), f32[8,16,256]{2,0,1:T(8,128)}) %all-reduce.2.cloned.1.call-update) | async-done | bytes 131088 | tf_op jit(solution)/shard_map/psum | solution.py:97
  347.8 1.6 copy.149
  (577 shorter events, 103.8 us)
Async XLA Ops:
  7.2 340.7 %all-reduce.2.cloned.1.call-start = ((), (), s32[]{:S(2)}) async-start(), calls=%async_computation | async-start | bytes 262144 | tf_op jit(solution)/shard_map/psum | solution.py:97
  10.3 3.3 copy-start.18
  13.6 24.8 %copy-start = (f32[1,2,3,8,16,256]{5,3,4,2,1,0:T(8,128)}, f32[1,2,3,8,16,256]{5,3,4,2,1,0:T(8,128)S(1)}, u32[]{:S(2)}) copy-start(f32[1,2,3,8,16,256]{5,3,4,2,1,0:T(8,128)S(1)} %get-tuple-element.705) | copy-start | bytes 2359300 | tf_op jit(solution)/shard_map/while
  20.9 6.7 %collective-permute-start = (f32[2,8,1,256]{3,1,2,0:T(8,128)}, f32[2,8,1,256]{3,1,2,0:T(8,128)}, u32[]{:S(2)}, u32[]{:S(2)}) collective-permute-start(f32[2,8,1,256]{3,1,2,0:T(8,128)} %get-tuple-element.584), channel_id=1, source_target_pairs={{1,0},{2,1},{3,2},{5,4},{6,5},{7,6},{9,8},{10,9},{11,10},{13,12},{... | collective-permute-start | bytes 49160 | tf_op jit(solution)/shard_map/while/body/eval_jaxpr/ppermute | solution.py:19
  22.2 5.4 %collective-permute-start.1 = (f32[2,8,1,256]{3,1,2,0:T(8,128)}, f32[2,8,1,256]{3,1,2,0:T(8,128)}, u32[]{:S(2)}, u32[]{:S(2)}) collective-permute-start(f32[2,8,1,256]{3,1,2,0:T(8,128)} %get-tuple-element.585), channel_id=1, source_target_pairs={{0,1},{1,2},{2,3},{4,5},{5,6},{6,7},{8,9},{9,10},{10,11},{12,13},{... | collective-permute-start | bytes 49160 | tf_op jit(solution)/shard_map/while/body/eval_jaxpr/ppermute | solution.py:18
  30.1 5.8 %collective-permute-start.2 = (f32[2,8,1,256]{3,1,2,0:T(8,128)S(1)}, f32[2,8,1,256]{3,1,2,0:T(8,128)S(1)}, u32[]{:S(2)}, u32[]{:S(2)}) collective-permute-start(f32[2,8,1,256]{3,1,2,0:T(8,128)S(1)} %get-tuple-element.600), channel_id=1, source_target_pairs={{1,0},{2,1},{3,2},{5,4},{6,5},{7,6},{9,8},{10,9},{11,10},{13,12},{... | collective-permute-start | bytes 49160 | tf_op jit(solution)/shard_map/while/body/eval_jaxpr/ppermute | solution.py:19
  31.4 5.4 %collective-permute-start.3 = (f32[2,8,1,256]{3,1,2,0:T(8,128)S(1)}, f32[2,8,1,256]{3,1,2,0:T(8,128)S(1)}, u32[]{:S(2)}, u32[]{:S(2)}) collective-permute-start(f32[2,8,1,256]{3,1,2,0:T(8,128)S(1)} %get-tuple-element.601), channel_id=1, source_target_pairs={{0,1},{1,2},{2,3},{4,5},{5,6},{6,7},{8,9},{9,10},{10,11},{12,13},{... | collective-permute-start | bytes 49160 | tf_op jit(solution)/shard_map/while/body/eval_jaxpr/ppermute | solution.py:18
  38.5 5.6 %collective-permute-start.4 = (f32[2,8,1,256]{3,1,2,0:T(8,128)S(1)}, f32[2,8,1,256]{3,1,2,0:T(8,128)S(1)}, u32[]{:S(2)}, u32[]{:S(2)}) collective-permute-start(f32[2,8,1,256]{3,1,2,0:T(8,128)S(1)} %get-tuple-element.616), channel_id=1, source_target_pairs={{1,0},{2,1},{3,2},{5,4},{6,5},{7,6},{9,8},{10,9},{11,10},{13,12},{... | collective-permute-start | bytes 49160 | tf_op jit(solution)/shard_map/while/body/eval_jaxpr/ppermute | solution.py:19
  39.8 5.1 %collective-permute-start.5 = (f32[2,8,1,256]{3,1,2,0:T(8,128)S(1)}, f32[2,8,1,256]{3,1,2,0:T(8,128)S(1)}, u32[]{:S(2)}, u32[]{:S(2)}) collective-permute-start(f32[2,8,1,256]{3,1,2,0:T(8,128)S(1)} %get-tuple-element.617), channel_id=1, source_target_pairs={{0,1},{1,2},{2,3},{4,5},{5,6},{6,7},{8,9},{9,10},{10,11},{12,13},{... | collective-permute-start | bytes 49160 | tf_op jit(solution)/shard_map/while/body/eval_jaxpr/ppermute | solution.py:18
  51.8 6.8 %collective-permute-start.6 = (f32[2,8,1,256]{3,1,2,0:T(8,128)S(1)}, f32[2,8,1,256]{3,1,2,0:T(8,128)S(1)}, u32[]{:S(2)}, u32[]{:S(2)}) collective-permute-start(f32[2,8,1,256]{3,1,2,0:T(8,128)S(1)} %get-tuple-element.634), channel_id=1, source_target_pairs={{1,0},{2,1},{3,2},{5,4},{6,5},{7,6},{9,8},{10,9},{11,10},{13,12},{... | collective-permute-start | bytes 49160 | tf_op jit(solution)/shard_map/while/body/eval_jaxpr/ppermute | solution.py:19
  53.1 5.7 %collective-permute-start.7 = (f32[2,8,1,256]{3,1,2,0:T(8,128)S(1)}, f32[2,8,1,256]{3,1,2,0:T(8,128)S(1)}, u32[]{:S(2)}, u32[]{:S(2)}) collective-permute-start(f32[2,8,1,256]{3,1,2,0:T(8,128)S(1)} %get-tuple-element.635), channel_id=1, source_target_pairs={{0,1},{1,2},{2,3},{4,5},{5,6},{6,7},{8,9},{9,10},{10,11},{12,13},{... | collective-permute-start | bytes 49160 | tf_op jit(solution)/shard_map/while/body/eval_jaxpr/ppermute | solution.py:18
  58.0 1.6 copy-start.9
  58.0 1.6 copy-start.13
  60.7 6.2 %collective-permute-start.8 = (f32[2,8,1,256]{3,1,2,0:T(8,128)S(1)}, f32[2,8,1,256]{3,1,2,0:T(8,128)S(1)}, u32[]{:S(2)}, u32[]{:S(2)}) collective-permute-start(f32[2,8,1,256]{3,1,2,0:T(8,128)S(1)} %get-tuple-element.650), channel_id=1, source_target_pairs={{1,0},{2,1},{3,2},{5,4},{6,5},{7,6},{9,8},{10,9},{11,10},{13,12},{... | collective-permute-start | bytes 49160 | tf_op jit(solution)/shard_map/while/body/eval_jaxpr/ppermute | solution.py:19
  62.0 5.7 %collective-permute-start.9 = (f32[2,8,1,256]{3,1,2,0:T(8,128)S(1)}, f32[2,8,1,256]{3,1,2,0:T(8,128)S(1)}, u32[]{:S(2)}, u32[]{:S(2)}) collective-permute-start(f32[2,8,1,256]{3,1,2,0:T(8,128)S(1)} %get-tuple-element.651), channel_id=1, source_target_pairs={{0,1},{1,2},{2,3},{4,5},{5,6},{6,7},{8,9},{9,10},{10,11},{12,13},{... | collective-permute-start | bytes 49160 | tf_op jit(solution)/shard_map/while/body/eval_jaxpr/ppermute | solution.py:18
  69.5 6.2 %collective-permute-start.10 = (f32[2,8,1,256]{3,1,2,0:T(8,128)S(1)}, f32[2,8,1,256]{3,1,2,0:T(8,128)S(1)}, u32[]{:S(2)}, u32[]{:S(2)}) collective-permute-start(f32[2,8,1,256]{3,1,2,0:T(8,128)S(1)} %get-tuple-element.666), channel_id=1, source_target_pairs={{1,0},{2,1},{3,2},{5,4},{6,5},{7,6},{9,8},{10,9},{11,10},{13,12},{... | collective-permute-start | bytes 49160 | tf_op jit(solution)/shard_map/while/body/eval_jaxpr/ppermute | solution.py:19
  70.8 5.7 %collective-permute-start.11 = (f32[2,8,1,256]{3,1,2,0:T(8,128)S(1)}, f32[2,8,1,256]{3,1,2,0:T(8,128)S(1)}, u32[]{:S(2)}, u32[]{:S(2)}) collective-permute-start(f32[2,8,1,256]{3,1,2,0:T(8,128)S(1)} %get-tuple-element.667), channel_id=1, source_target_pairs={{0,1},{1,2},{2,3},{4,5},{5,6},{6,7},{8,9},{9,10},{10,11},{12,13},{... | collective-permute-start | bytes 49160 | tf_op jit(solution)/shard_map/while/body/eval_jaxpr/ppermute | solution.py:18
  78.2 12.5 %collective-permute-start.12 = (f32[3,8,16,256]{3,1,2,0:T(8,128)S(1)}, f32[3,8,16,256]{3,1,2,0:T(8,128)S(1)}, u32[]{:S(2)}, u32[]{:S(2)}) collective-permute-start(f32[3,8,16,256]{3,1,2,0:T(8,128)S(1)} %fusion.480), channel_id=1, source_target_pairs={{4,0},{8,4},{12,8},{5,1},{9,5},{13,9},{6,2},{10,6},{14,10},{7,3},{... | collective-permute-start | bytes 1179656 | tf_op jit(solution)/shard_map/while/body/eval_jaxpr/ppermute | solution.py:27
  90.7 25.3 %copy-start = (f32[1,2,3,8,16,256]{5,3,4,2,1,0:T(8,128)}, f32[1,2,3,8,16,256]{5,3,4,2,1,0:T(8,128)S(1)}, u32[]{:S(2)}) copy-start(f32[1,2,3,8,16,256]{5,3,4,2,1,0:T(8,128)S(1)} %get-tuple-element.705) | copy-start | bytes 2359300 | tf_op jit(solution)/shard_map/while
  97.9 7.4 %collective-permute-start = (f32[2,8,1,256]{3,1,2,0:T(8,128)}, f32[2,8,1,256]{3,1,2,0:T(8,128)}, u32[]{:S(2)}, u32[]{:S(2)}) collective-permute-start(f32[2,8,1,256]{3,1,2,0:T(8,128)} %get-tuple-element.584), channel_id=1, source_target_pairs={{1,0},{2,1},{3,2},{5,4},{6,5},{7,6},{9,8},{10,9},{11,10},{13,12},{... | collective-permute-start | bytes 49160 | tf_op jit(solution)/shard_map/while/body/eval_jaxpr/ppermute | solution.py:19
  99.2 6.1 %collective-permute-start.1 = (f32[2,8,1,256]{3,1,2,0:T(8,128)}, f32[2,8,1,256]{3,1,2,0:T(8,128)}, u32[]{:S(2)}, u32[]{:S(2)}) collective-permute-start(f32[2,8,1,256]{3,1,2,0:T(8,128)} %get-tuple-element.585), channel_id=1, source_target_pairs={{0,1},{1,2},{2,3},{4,5},{5,6},{6,7},{8,9},{9,10},{10,11},{12,13},{... | collective-permute-start | bytes 49160 | tf_op jit(solution)/shard_map/while/body/eval_jaxpr/ppermute | solution.py:18
  107.8 5.6 %collective-permute-start.2 = (f32[2,8,1,256]{3,1,2,0:T(8,128)S(1)}, f32[2,8,1,256]{3,1,2,0:T(8,128)S(1)}, u32[]{:S(2)}, u32[]{:S(2)}) collective-permute-start(f32[2,8,1,256]{3,1,2,0:T(8,128)S(1)} %get-tuple-element.600), channel_id=1, source_target_pairs={{1,0},{2,1},{3,2},{5,4},{6,5},{7,6},{9,8},{10,9},{11,10},{13,12},{... | collective-permute-start | bytes 49160 | tf_op jit(solution)/shard_map/while/body/eval_jaxpr/ppermute | solution.py:19
  109.1 5.1 %collective-permute-start.3 = (f32[2,8,1,256]{3,1,2,0:T(8,128)S(1)}, f32[2,8,1,256]{3,1,2,0:T(8,128)S(1)}, u32[]{:S(2)}, u32[]{:S(2)}) collective-permute-start(f32[2,8,1,256]{3,1,2,0:T(8,128)S(1)} %get-tuple-element.601), channel_id=1, source_target_pairs={{0,1},{1,2},{2,3},{4,5},{5,6},{6,7},{8,9},{9,10},{10,11},{12,13},{... | collective-permute-start | bytes 49160 | tf_op jit(solution)/shard_map/while/body/eval_jaxpr/ppermute | solution.py:18
  116.0 5.6 %collective-permute-start.4 = (f32[2,8,1,256]{3,1,2,0:T(8,128)S(1)}, f32[2,8,1,256]{3,1,2,0:T(8,128)S(1)}, u32[]{:S(2)}, u32[]{:S(2)}) collective-permute-start(f32[2,8,1,256]{3,1,2,0:T(8,128)S(1)} %get-tuple-element.616), channel_id=1, source_target_pairs={{1,0},{2,1},{3,2},{5,4},{6,5},{7,6},{9,8},{10,9},{11,10},{13,12},{... | collective-permute-start | bytes 49160 | tf_op jit(solution)/shard_map/while/body/eval_jaxpr/ppermute | solution.py:19
  117.3 5.1 %collective-permute-start.5 = (f32[2,8,1,256]{3,1,2,0:T(8,128)S(1)}, f32[2,8,1,256]{3,1,2,0:T(8,128)S(1)}, u32[]{:S(2)}, u32[]{:S(2)}) collective-permute-start(f32[2,8,1,256]{3,1,2,0:T(8,128)S(1)} %get-tuple-element.617), channel_id=1, source_target_pairs={{0,1},{1,2},{2,3},{4,5},{5,6},{6,7},{8,9},{9,10},{10,11},{12,13},{... | collective-permute-start | bytes 49160 | tf_op jit(solution)/shard_map/while/body/eval_jaxpr/ppermute | solution.py:18
  129.3 6.8 %collective-permute-start.6 = (f32[2,8,1,256]{3,1,2,0:T(8,128)S(1)}, f32[2,8,1,256]{3,1,2,0:T(8,128)S(1)}, u32[]{:S(2)}, u32[]{:S(2)}) collective-permute-start(f32[2,8,1,256]{3,1,2,0:T(8,128)S(1)} %get-tuple-element.634), channel_id=1, source_target_pairs={{1,0},{2,1},{3,2},{5,4},{6,5},{7,6},{9,8},{10,9},{11,10},{13,12},{... | collective-permute-start | bytes 49160 | tf_op jit(solution)/shard_map/while/body/eval_jaxpr/ppermute | solution.py:19
  130.6 5.7 %collective-permute-start.7 = (f32[2,8,1,256]{3,1,2,0:T(8,128)S(1)}, f32[2,8,1,256]{3,1,2,0:T(8,128)S(1)}, u32[]{:S(2)}, u32[]{:S(2)}) collective-permute-start(f32[2,8,1,256]{3,1,2,0:T(8,128)S(1)} %get-tuple-element.635), channel_id=1, source_target_pairs={{0,1},{1,2},{2,3},{4,5},{5,6},{6,7},{8,9},{9,10},{10,11},{12,13},{... | collective-permute-start | bytes 49160 | tf_op jit(solution)/shard_map/while/body/eval_jaxpr/ppermute | solution.py:18
  135.5 1.6 copy-start.9
  138.3 6.2 %collective-permute-start.8 = (f32[2,8,1,256]{3,1,2,0:T(8,128)S(1)}, f32[2,8,1,256]{3,1,2,0:T(8,128)S(1)}, u32[]{:S(2)}, u32[]{:S(2)}) collective-permute-start(f32[2,8,1,256]{3,1,2,0:T(8,128)S(1)} %get-tuple-element.650), channel_id=1, source_target_pairs={{1,0},{2,1},{3,2},{5,4},{6,5},{7,6},{9,8},{10,9},{11,10},{13,12},{... | collective-permute-start | bytes 49160 | tf_op jit(solution)/shard_map/while/body/eval_jaxpr/ppermute | solution.py:19
  139.6 5.7 %collective-permute-start.9 = (f32[2,8,1,256]{3,1,2,0:T(8,128)S(1)}, f32[2,8,1,256]{3,1,2,0:T(8,128)S(1)}, u32[]{:S(2)}, u32[]{:S(2)}) collective-permute-start(f32[2,8,1,256]{3,1,2,0:T(8,128)S(1)} %get-tuple-element.651), channel_id=1, source_target_pairs={{0,1},{1,2},{2,3},{4,5},{5,6},{6,7},{8,9},{9,10},{10,11},{12,13},{... | collective-permute-start | bytes 49160 | tf_op jit(solution)/shard_map/while/body/eval_jaxpr/ppermute | solution.py:18
  147.0 6.2 %collective-permute-start.10 = (f32[2,8,1,256]{3,1,2,0:T(8,128)S(1)}, f32[2,8,1,256]{3,1,2,0:T(8,128)S(1)}, u32[]{:S(2)}, u32[]{:S(2)}) collective-permute-start(f32[2,8,1,256]{3,1,2,0:T(8,128)S(1)} %get-tuple-element.666), channel_id=1, source_target_pairs={{1,0},{2,1},{3,2},{5,4},{6,5},{7,6},{9,8},{10,9},{11,10},{13,12},{... | collective-permute-start | bytes 49160 | tf_op jit(solution)/shard_map/while/body/eval_jaxpr/ppermute | solution.py:19
  148.3 5.7 %collective-permute-start.11 = (f32[2,8,1,256]{3,1,2,0:T(8,128)S(1)}, f32[2,8,1,256]{3,1,2,0:T(8,128)S(1)}, u32[]{:S(2)}, u32[]{:S(2)}) collective-permute-start(f32[2,8,1,256]{3,1,2,0:T(8,128)S(1)} %get-tuple-element.667), channel_id=1, source_target_pairs={{0,1},{1,2},{2,3},{4,5},{5,6},{6,7},{8,9},{9,10},{10,11},{12,13},{... | collective-permute-start | bytes 49160 | tf_op jit(solution)/shard_map/while/body/eval_jaxpr/ppermute | solution.py:18
  155.7 12.5 %collective-permute-start.12 = (f32[3,8,16,256]{3,1,2,0:T(8,128)S(1)}, f32[3,8,16,256]{3,1,2,0:T(8,128)S(1)}, u32[]{:S(2)}, u32[]{:S(2)}) collective-permute-start(f32[3,8,16,256]{3,1,2,0:T(8,128)S(1)} %fusion.480), channel_id=1, source_target_pairs={{4,0},{8,4},{12,8},{5,1},{9,5},{13,9},{6,2},{10,6},{14,10},{7,3},{... | collective-permute-start | bytes 1179656 | tf_op jit(solution)/shard_map/while/body/eval_jaxpr/ppermute | solution.py:27
  168.2 25.3 %copy-start = (f32[1,2,3,8,16,256]{5,3,4,2,1,0:T(8,128)}, f32[1,2,3,8,16,256]{5,3,4,2,1,0:T(8,128)S(1)}, u32[]{:S(2)}) copy-start(f32[1,2,3,8,16,256]{5,3,4,2,1,0:T(8,128)S(1)} %get-tuple-element.705) | copy-start | bytes 2359300 | tf_op jit(solution)/shard_map/while
  175.5 7.4 %collective-permute-start = (f32[2,8,1,256]{3,1,2,0:T(8,128)}, f32[2,8,1,256]{3,1,2,0:T(8,128)}, u32[]{:S(2)}, u32[]{:S(2)}) collective-permute-start(f32[2,8,1,256]{3,1,2,0:T(8,128)} %get-tuple-element.584), channel_id=1, source_target_pairs={{1,0},{2,1},{3,2},{5,4},{6,5},{7,6},{9,8},{10,9},{11,10},{13,12},{... | collective-permute-start | bytes 49160 | tf_op jit(solution)/shard_map/while/body/eval_jaxpr/ppermute | solution.py:19
  176.7 6.1 %collective-permute-start.1 = (f32[2,8,1,256]{3,1,2,0:T(8,128)}, f32[2,8,1,256]{3,1,2,0:T(8,128)}, u32[]{:S(2)}, u32[]{:S(2)}) collective-permute-start(f32[2,8,1,256]{3,1,2,0:T(8,128)} %get-tuple-element.585), channel_id=1, source_target_pairs={{0,1},{1,2},{2,3},{4,5},{5,6},{6,7},{8,9},{9,10},{10,11},{12,13},{... | collective-permute-start | bytes 49160 | tf_op jit(solution)/shard_map/while/body/eval_jaxpr/ppermute | solution.py:18
  185.4 5.6 %collective-permute-start.2 = (f32[2,8,1,256]{3,1,2,0:T(8,128)S(1)}, f32[2,8,1,256]{3,1,2,0:T(8,128)S(1)}, u32[]{:S(2)}, u32[]{:S(2)}) collective-permute-start(f32[2,8,1,256]{3,1,2,0:T(8,128)S(1)} %get-tuple-element.600), channel_id=1, source_target_pairs={{1,0},{2,1},{3,2},{5,4},{6,5},{7,6},{9,8},{10,9},{11,10},{13,12},{... | collective-permute-start | bytes 49160 | tf_op jit(solution)/shard_map/while/body/eval_jaxpr/ppermute | solution.py:19
  186.7 5.1 %collective-permute-start.3 = (f32[2,8,1,256]{3,1,2,0:T(8,128)S(1)}, f32[2,8,1,256]{3,1,2,0:T(8,128)S(1)}, u32[]{:S(2)}, u32[]{:S(2)}) collective-permute-start(f32[2,8,1,256]{3,1,2,0:T(8,128)S(1)} %get-tuple-element.601), channel_id=1, source_target_pairs={{0,1},{1,2},{2,3},{4,5},{5,6},{6,7},{8,9},{9,10},{10,11},{12,13},{... | collective-permute-start | bytes 49160 | tf_op jit(solution)/shard_map/while/body/eval_jaxpr/ppermute | solution.py:18
  193.5 5.6 %collective-permute-start.4 = (f32[2,8,1,256]{3,1,2,0:T(8,128)S(1)}, f32[2,8,1,256]{3,1,2,0:T(8,128)S(1)}, u32[]{:S(2)}, u32[]{:S(2)}) collective-permute-start(f32[2,8,1,256]{3,1,2,0:T(8,128)S(1)} %get-tuple-element.616), channel_id=1, source_target_pairs={{1,0},{2,1},{3,2},{5,4},{6,5},{7,6},{9,8},{10,9},{11,10},{13,12},{... | collective-permute-start | bytes 49160 | tf_op jit(solution)/shard_map/while/body/eval_jaxpr/ppermute | solution.py:19
  194.8 5.1 %collective-permute-start.5 = (f32[2,8,1,256]{3,1,2,0:T(8,128)S(1)}, f32[2,8,1,256]{3,1,2,0:T(8,128)S(1)}, u32[]{:S(2)}, u32[]{:S(2)}) collective-permute-start(f32[2,8,1,256]{3,1,2,0:T(8,128)S(1)} %get-tuple-element.617), channel_id=1, source_target_pairs={{0,1},{1,2},{2,3},{4,5},{5,6},{6,7},{8,9},{9,10},{10,11},{12,13},{... | collective-permute-start | bytes 49160 | tf_op jit(solution)/shard_map/while/body/eval_jaxpr/ppermute | solution.py:18
  206.8 6.8 %collective-permute-start.6 = (f32[2,8,1,256]{3,1,2,0:T(8,128)S(1)}, f32[2,8,1,256]{3,1,2,0:T(8,128)S(1)}, u32[]{:S(2)}, u32[]{:S(2)}) collective-permute-start(f32[2,8,1,256]{3,1,2,0:T(8,128)S(1)} %get-tuple-element.634), channel_id=1, source_target_pairs={{1,0},{2,1},{3,2},{5,4},{6,5},{7,6},{9,8},{10,9},{11,10},{13,12},{... | collective-permute-start | bytes 49160 | tf_op jit(solution)/shard_map/while/body/eval_jaxpr/ppermute | solution.py:19
  208.1 5.7 %collective-permute-start.7 = (f32[2,8,1,256]{3,1,2,0:T(8,128)S(1)}, f32[2,8,1,256]{3,1,2,0:T(8,128)S(1)}, u32[]{:S(2)}, u32[]{:S(2)}) collective-permute-start(f32[2,8,1,256]{3,1,2,0:T(8,128)S(1)} %get-tuple-element.635), channel_id=1, source_target_pairs={{0,1},{1,2},{2,3},{4,5},{5,6},{6,7},{8,9},{9,10},{10,11},{12,13},{... | collective-permute-start | bytes 49160 | tf_op jit(solution)/shard_map/while/body/eval_jaxpr/ppermute | solution.py:18
  213.0 1.6 copy-start.9
  215.8 6.2 %collective-permute-start.8 = (f32[2,8,1,256]{3,1,2,0:T(8,128)S(1)}, f32[2,8,1,256]{3,1,2,0:T(8,128)S(1)}, u32[]{:S(2)}, u32[]{:S(2)}) collective-permute-start(f32[2,8,1,256]{3,1,2,0:T(8,128)S(1)} %get-tuple-element.650), channel_id=1, source_target_pairs={{1,0},{2,1},{3,2},{5,4},{6,5},{7,6},{9,8},{10,9},{11,10},{13,12},{... | collective-permute-start | bytes 49160 | tf_op jit(solution)/shard_map/while/body/eval_jaxpr/ppermute | solution.py:19
  217.1 5.7 %collective-permute-start.9 = (f32[2,8,1,256]{3,1,2,0:T(8,128)S(1)}, f32[2,8,1,256]{3,1,2,0:T(8,128)S(1)}, u32[]{:S(2)}, u32[]{:S(2)}) collective-permute-start(f32[2,8,1,256]{3,1,2,0:T(8,128)S(1)} %get-tuple-element.651), channel_id=1, source_target_pairs={{0,1},{1,2},{2,3},{4,5},{5,6},{6,7},{8,9},{9,10},{10,11},{12,13},{... | collective-permute-start | bytes 49160 | tf_op jit(solution)/shard_map/while/body/eval_jaxpr/ppermute | solution.py:18
  224.5 6.2 %collective-permute-start.10 = (f32[2,8,1,256]{3,1,2,0:T(8,128)S(1)}, f32[2,8,1,256]{3,1,2,0:T(8,128)S(1)}, u32[]{:S(2)}, u32[]{:S(2)}) collective-permute-start(f32[2,8,1,256]{3,1,2,0:T(8,128)S(1)} %get-tuple-element.666), channel_id=1, source_target_pairs={{1,0},{2,1},{3,2},{5,4},{6,5},{7,6},{9,8},{10,9},{11,10},{13,12},{... | collective-permute-start | bytes 49160 | tf_op jit(solution)/shard_map/while/body/eval_jaxpr/ppermute | solution.py:19
  225.8 5.7 %collective-permute-start.11 = (f32[2,8,1,256]{3,1,2,0:T(8,128)S(1)}, f32[2,8,1,256]{3,1,2,0:T(8,128)S(1)}, u32[]{:S(2)}, u32[]{:S(2)}) collective-permute-start(f32[2,8,1,256]{3,1,2,0:T(8,128)S(1)} %get-tuple-element.667), channel_id=1, source_target_pairs={{0,1},{1,2},{2,3},{4,5},{5,6},{6,7},{8,9},{9,10},{10,11},{12,13},{... | collective-permute-start | bytes 49160 | tf_op jit(solution)/shard_map/while/body/eval_jaxpr/ppermute | solution.py:18
  233.2 12.5 %collective-permute-start.12 = (f32[3,8,16,256]{3,1,2,0:T(8,128)S(1)}, f32[3,8,16,256]{3,1,2,0:T(8,128)S(1)}, u32[]{:S(2)}, u32[]{:S(2)}) collective-permute-start(f32[3,8,16,256]{3,1,2,0:T(8,128)S(1)} %fusion.480), channel_id=1, source_target_pairs={{4,0},{8,4},{12,8},{5,1},{9,5},{13,9},{6,2},{10,6},{14,10},{7,3},{... | collective-permute-start | bytes 1179656 | tf_op jit(solution)/shard_map/while/body/eval_jaxpr/ppermute | solution.py:27
  250.1 4.5 %copy-start.14 = (f32[1,8,16,256]{3,1,2,0:T(8,128)}, f32[1,8,16,256]{3,1,2,0:T(8,128)S(1)}, u32[]{:S(2)}) copy-start(f32[1,8,16,256]{3,1,2,0:T(8,128)S(1)} %get-tuple-element.419) | copy-start | bytes 393220
  250.1 5.7 %collective-permute-start.13 = (f32[2,8,1,256]{3,1,2,0:T(8,128)S(1)}, f32[2,8,1,256]{3,1,2,0:T(8,128)S(1)}, u32[]{:S(2)}, u32[]{:S(2)}) collective-permute-start(f32[2,8,1,256]{3,1,2,0:T(8,128)S(1)} %get-tuple-element.367), channel_id=1, source_target_pairs={{0,1},{1,2},{2,3},{4,5},{5,6},{6,7},{8,9},{9,10},{10,11},{12,13},{... | collective-permute-start | bytes 49160 | tf_op jit(solution)/shard_map/ppermute | solution.py:18
  253.3 4.9 %collective-permute-start.14 = (f32[2,8,1,256]{3,1,2,0:T(8,128)S(1)}, f32[2,8,1,256]{3,1,2,0:T(8,128)S(1)}, u32[]{:S(2)}, u32[]{:S(2)}) collective-permute-start(f32[2,8,1,256]{3,1,2,0:T(8,128)S(1)} %get-tuple-element.368), channel_id=1, source_target_pairs={{1,0},{2,1},{3,2},{5,4},{6,5},{7,6},{9,8},{10,9},{11,10},{13,12},{... | collective-permute-start | bytes 49160 | tf_op jit(solution)/shard_map/ppermute | solution.py:19
  254.6 5.3 %copy-start.10 = (f32[8,1,1]{0,2,1:T(1,128)S(1)}, f32[8,1,1]{0,2,1:T(1,128)}, u32[]{:S(2)}) copy-start(f32[8,1,1]{0,2,1:T(1,128)} %get-tuple-element.715) | copy-start | bytes 100
  260.8 5.7 %collective-permute-start.15 = (f32[2,8,1,256]{3,1,2,0:T(8,128)S(1)}, f32[2,8,1,256]{3,1,2,0:T(8,128)S(1)}, u32[]{:S(2)}, u32[]{:S(2)}) collective-permute-start(f32[2,8,1,256]{3,1,2,0:T(8,128)S(1)} %get-tuple-element.365), channel_id=1, source_target_pairs={{0,1},{1,2},{2,3},{4,5},{5,6},{6,7},{8,9},{9,10},{10,11},{12,13},{... | collective-permute-start | bytes 49160 | tf_op jit(solution)/shard_map/ppermute | solution.py:18
  265.2 3.1 collective-permute-start.16
  270.0 5.2 %collective-permute-start.17 = (f32[2,8,1,256]{3,1,2,0:T(8,128)S(1)}, f32[2,8,1,256]{3,1,2,0:T(8,128)S(1)}, u32[]{:S(2)}, u32[]{:S(2)}) collective-permute-start(f32[2,8,1,256]{3,1,2,0:T(8,128)S(1)} %get-tuple-element.363), channel_id=1, source_target_pairs={{0,1},{1,2},{2,3},{4,5},{5,6},{6,7},{8,9},{9,10},{10,11},{12,13},{... | collective-permute-start | bytes 49160 | tf_op jit(solution)/shard_map/ppermute | solution.py:18
  273.9 3.1 collective-permute-start.18
  280.1 3.5 copy-start.6
  283.7 18.8 %copy-start.4 = (f32[3,8,16,256]{3,1,2,0:T(8,128)}, f32[3,8,16,256]{3,1,2,0:T(8,128)S(1)}, u32[]{:S(2)}) copy-start(f32[3,8,16,256]{3,1,2,0:T(8,128)S(1)} %get-tuple-element.406) | copy-start | bytes 1179652
  284.3 6.4 %collective-permute-start.19 = (f32[2,8,1,256]{3,1,2,0:T(8,128)S(1)}, f32[2,8,1,256]{3,1,2,0:T(8,128)S(1)}, u32[]{:S(2)}, u32[]{:S(2)}) collective-permute-start(f32[2,8,1,256]{3,1,2,0:T(8,128)S(1)} %get-tuple-element.361), channel_id=1, source_target_pairs={{0,1},{1,2},{2,3},{4,5},{5,6},{6,7},{8,9},{9,10},{10,11},{12,13},{... | collective-permute-start | bytes 49160 | tf_op jit(solution)/shard_map/ppermute | solution.py:18
  288.2 3.1 collective-permute-start.20
  293.9 5.2 %collective-permute-start.21 = (f32[2,8,1,256]{3,1,2,0:T(8,128)S(1)}, f32[2,8,1,256]{3,1,2,0:T(8,128)S(1)}, u32[]{:S(2)}, u32[]{:S(2)}) collective-permute-start(f32[2,8,1,256]{3,1,2,0:T(8,128)S(1)} %get-tuple-element.359), channel_id=1, source_target_pairs={{0,1},{1,2},{2,3},{4,5},{5,6},{6,7},{8,9},{9,10},{10,11},{12,13},{... | collective-permute-start | bytes 49160 | tf_op jit(solution)/shard_map/ppermute | solution.py:18
  297.8 3.1 collective-permute-start.22
  302.6 5.2 %collective-permute-start.23 = (f32[2,8,1,256]{3,1,2,0:T(8,128)S(1)}, f32[2,8,1,256]{3,1,2,0:T(8,128)S(1)}, u32[]{:S(2)}, u32[]{:S(2)}) collective-permute-start(f32[2,8,1,256]{3,1,2,0:T(8,128)S(1)} %get-tuple-element.357), channel_id=1, source_target_pairs={{0,1},{1,2},{2,3},{4,5},{5,6},{6,7},{8,9},{9,10},{10,11},{12,13},{... | collective-permute-start | bytes 49160 | tf_op jit(solution)/shard_map/ppermute | solution.py:18
  306.6 3.1 collective-permute-start.24
  (29 other events, 35.4 us)
Sparse Core Ops, SparseCore 0:
  312.4 35.3 all-reduce.1
where the time goes:
time: 359 us; the launch traced here: 356 us
  starting transfers between devices  140 us (39%)
  waiting for transfers between devices  88.5 us (25%)
  local copies, waits for them, and re-layouts  51.5 us (14%)
  other arithmetic  50.6 us (14%)
  between operations  14.9 us (4%)
  matrix products  8.32 us (2%)
    ppermute x24, starting transfers between devices, with_halo(): before = lax.ppermute(last, axis, up)  105 us
    psum x1, waiting for transfers between devices, per_device(): total_bias = lax.psum(bias, 'win')  34.5 us
    ppermute x3, waiting for transfers between devices, passed_along(): lax.ppermute(value, axis, [(source, source + steps) for source in range(i...  33.5 us
    ppermute x24, starting transfers between devices, with_halo(): after = lax.ppermute(initial, axis, down)  31 us
    scatter-add x8, other arithmetic, add_obs(): layer_a.reshape(layer_a.shape[0], -1).at[:, cells].add(values[None, :])  23.2 us
    ppermute x24, waiting for transfers between devices, with_halo(): before = lax.ppermute(last, axis, up)  10.4 us
    ppermute x24, waiting for transfers between devices, with_halo(): after = lax.ppermute(initial, axis, down)  10 us
    dot_general x24, matrix products, tendency(): jnp.einsum('kl,krc->lrc', mix, dxp + dyq, precision=lax.Precision.HIGHEST)  8.32 us
  transfers between devices with their start and end apart: 52, of which 25 were waited for; matrix products, arithmetic and copies ran while one was open for 3% of the time, Pallas kernels for 0%

commit v1 on v0

--- a/solution.py
+++ b/solution.py
@@ -94,7 +94,7 @@
 
     incoming = lax.fori_loop(0, rounds, relay_round, zero_state)
     lam, bias = integrate(incoming)
-    total_bias = lax.psum(bias, "win")
+    total_bias = jnp.sum(lax.all_gather(bias, "win"), axis=0)
     return (lam[None], total_bias)
 
 

time: 359 us -> 326 us (0.908)
  waiting for transfers between devices: 88.5 us -> 54 us
  blocking collectives: 0 us -> 15.9 us
  between operations: 14.9 us -> 1.51 us
    psum x1 -> x0, waiting for transfers between devices: 34.5 us -> none  [per_device(): total_bias = lax.psum(bias, 'win')]
    all_gather x0 -> x1, blocking collectives: none -> 15.9 us  [per_device(): total_bias = jnp.sum(lax.all_gather(bias, 'win'), axis=0)]
  transfers between devices with their start and end apart: 52 -> 51, of which waited for: 25 -> 24; matrix products, arithmetic and copies ran while one was open for 3% -> 3% of each run, Pallas kernels for 0% -> 0%
where the time goes in v1:
time: 326 us; the launch traced here: 323 us
  starting transfers between devices  140 us (43%)
  waiting for transfers between devices  54 us (17%)
  other arithmetic  50.7 us (16%)
  local copies, waits for them, and re-layouts  50.2 us (15%)
  blocking collectives  15.9 us (5%)
  matrix products  8.31 us (3%)
    ppermute x24, starting transfers between devices, with_halo(): before = lax.ppermute(last, axis, up)  105 us
    ppermute x3, waiting for transfers between devices, passed_along(): lax.ppermute(value, axis, [(source, source + steps) for source in range(i...  33.5 us
    ppermute x24, starting transfers between devices, with_halo(): after = lax.ppermute(initial, axis, down)  31 us
    scatter-add x8, other arithmetic, add_obs(): layer_a.reshape(layer_a.shape[0], -1).at[:, cells].add(values[None, :])  23.2 us
    all_gather x1, blocking collectives, per_device(): total_bias = jnp.sum(lax.all_gather(bias, 'win'), axis=0)  15.9 us
    ppermute x24, waiting for transfers between devices, with_halo(): before = lax.ppermute(last, axis, up)  10.4 us
    ppermute x24, waiting for transfers between devices, with_halo(): after = lax.ppermute(initial, axis, down)  10 us
    dot_general x24, matrix products, tendency(): jnp.einsum('kl,krc->lrc', mix, dxp + dyq, precision=lax.Precision.HIGHEST)  8.31 us
  transfers between devices with their start and end apart: 51, of which 24 were waited for; matrix products, arithmetic and copies ran while one was open for 3% of the time, Pallas kernels for 0%

profile of v1, /device:TPU:0, one launch (start us, length us, event | category | flops | bytes accessed | tf_op | source)
XLA Modules:
  0.0 323.1 jit_solution(6238025057490587434)
XLA Ops:
  1.4 1.6 copy.185
  4.3 1.3 compare_select_fusion.2
  5.6 1.3 fusion.376
  7.0 232.0 %while.17 = (s32[]{:T(128)}, f32[3,8,16,256]{3,1,2,0:T(8,128)S(1)}, s32[1,2,256]{2,1,0:T(2,128)}, f32[1,2,256]{2,1,0:T(2,128)}, f32[16,256]{1,0:T(8,128)S(1)}, /...) while((s32[]{:T(128)}, f32[3,8,16,256]{3,1,2,0:T(8,128)S(1)}, ...), condition=%wide.region_3.4_spmd.clone, body=%wide.region_0.3_spmd.clone.sunk | while | flops 31856224 | bytes 54825772 | solution.py:95
  7.1 1.4 compare_select_fusion.5
  8.4 1.3 fusion.443
  10.3 2.8 scatter_custom_fusion.16
  15.6 3.6 %collective-permute-start.1 = (f32[2,8,1,256]{3,1,2,0:T(8,128)}, f32[2,8,1,256]{3,1,2,0:T(8,128)}, u32[]{:S(2)}, u32[]{:S(2)}) collective-permute-start(f32[2,8,1,256]{3,1,2,0:T(8,128)} %get-tuple-element.596), channel_id=1, source_target_pairs={{0,1},{1,2},{2,3},{4,5},{5,6},{6,7},{8,9},{9,10},{10,11},{12,13},{... | collective-permute-start | bytes 49160 | tf_op jit(solution)/shard_map/while/body/eval_jaxpr/ppermute | solution.py:18
  23.5 1.3 collective-permute-start.2
  24.8 4.5 %collective-permute-start.3 = (f32[2,8,1,256]{3,1,2,0:T(8,128)S(1)}, f32[2,8,1,256]{3,1,2,0:T(8,128)S(1)}, u32[]{:S(2)}, u32[]{:S(2)}) collective-permute-start(f32[2,8,1,256]{3,1,2,0:T(8,128)S(1)} %get-tuple-element.612), channel_id=1, source_target_pairs={{0,1},{1,2},{2,3},{4,5},{5,6},{6,7},{8,9},{9,10},{10,11},{12,13},{... | collective-permute-start | bytes 49160 | tf_op jit(solution)/shard_map/while/body/eval_jaxpr/ppermute | solution.py:18
  31.9 1.3 collective-permute-start.4
  33.2 4.3 %collective-permute-start.5 = (f32[2,8,1,256]{3,1,2,0:T(8,128)S(1)}, f32[2,8,1,256]{3,1,2,0:T(8,128)S(1)}, u32[]{:S(2)}, u32[]{:S(2)}) collective-permute-start(f32[2,8,1,256]{3,1,2,0:T(8,128)S(1)} %get-tuple-element.628), channel_id=1, source_target_pairs={{0,1},{1,2},{2,3},{4,5},{5,6},{6,7},{8,9},{9,10},{10,11},{12,13},{... | collective-permute-start | bytes 49160 | tf_op jit(solution)/shard_map/while/body/eval_jaxpr/ppermute | solution.py:18
  40.7 2.9 scatter_custom_fusion.17
  45.2 1.3 collective-permute-start.6
  46.5 4.9 %collective-permute-start.7 = (f32[2,8,1,256]{3,1,2,0:T(8,128)S(1)}, f32[2,8,1,256]{3,1,2,0:T(8,128)S(1)}, u32[]{:S(2)}, u32[]{:S(2)}) collective-permute-start(f32[2,8,1,256]{3,1,2,0:T(8,128)S(1)} %get-tuple-element.646), channel_id=1, source_target_pairs={{0,1},{1,2},{2,3},{4,5},{5,6},{6,7},{8,9},{9,10},{10,11},{12,13},{... | collective-permute-start | bytes 49160 | tf_op jit(solution)/shard_map/while/body/eval_jaxpr/ppermute | solution.py:18
  54.1 1.3 collective-permute-start.8
  55.4 4.9 %collective-permute-start.9 = (f32[2,8,1,256]{3,1,2,0:T(8,128)S(1)}, f32[2,8,1,256]{3,1,2,0:T(8,128)S(1)}, u32[]{:S(2)}, u32[]{:S(2)}) collective-permute-start(f32[2,8,1,256]{3,1,2,0:T(8,128)S(1)} %get-tuple-element.662), channel_id=1, source_target_pairs={{0,1},{1,2},{2,3},{4,5},{5,6},{6,7},{8,9},{9,10},{10,11},{12,13},{... | collective-permute-start | bytes 49160 | tf_op jit(solution)/shard_map/while/body/eval_jaxpr/ppermute | solution.py:18
  62.9 1.3 collective-permute-start.10
  64.2 4.9 %collective-permute-start.11 = (f32[2,8,1,256]{3,1,2,0:T(8,128)S(1)}, f32[2,8,1,256]{3,1,2,0:T(8,128)S(1)}, u32[]{:S(2)}, u32[]{:S(2)}) collective-permute-start(f32[2,8,1,256]{3,1,2,0:T(8,128)S(1)} %get-tuple-element.678), channel_id=1, source_target_pairs={{0,1},{1,2},{2,3},{4,5},{5,6},{6,7},{8,9},{9,10},{10,11},{12,13},{... | collective-permute-start | bytes 49160 | tf_op jit(solution)/shard_map/while/body/eval_jaxpr/ppermute | solution.py:18
  72.9 11.2 %collective-permute-done.12 = f32[3,8,16,256]{3,1,2,0:T(8,128)S(1)} collective-permute-done((f32[3,8,16,256]{3,1,2,0:T(8,128)S(1)}, f32[3,8,16,256]{3,1,2,0:T(8,128)S(1)}, u32[]{:S(2)}, u32[]{:S(2)}) %collective-permute-start.12) | collective-permute-done | bytes 393248 | tf_op jit(solution)/shard_map/while/body/eval_jaxpr/ppermute | solution.py:27
  84.1 1.3 compare_select_fusion.5
  85.4 1.3 fusion.443
  87.3 2.8 scatter_custom_fusion.16
  92.6 4.4 %collective-permute-start.1 = (f32[2,8,1,256]{3,1,2,0:T(8,128)}, f32[2,8,1,256]{3,1,2,0:T(8,128)}, u32[]{:S(2)}, u32[]{:S(2)}) collective-permute-start(f32[2,8,1,256]{3,1,2,0:T(8,128)} %get-tuple-element.596), channel_id=1, source_target_pairs={{0,1},{1,2},{2,3},{4,5},{5,6},{6,7},{8,9},{9,10},{10,11},{12,13},{... | collective-permute-start | bytes 49160 | tf_op jit(solution)/shard_map/while/body/eval_jaxpr/ppermute | solution.py:18
  101.2 1.3 collective-permute-start.2
  102.5 4.3 %collective-permute-start.3 = (f32[2,8,1,256]{3,1,2,0:T(8,128)S(1)}, f32[2,8,1,256]{3,1,2,0:T(8,128)S(1)}, u32[]{:S(2)}, u32[]{:S(2)}) collective-permute-start(f32[2,8,1,256]{3,1,2,0:T(8,128)S(1)} %get-tuple-element.612), channel_id=1, source_target_pairs={{0,1},{1,2},{2,3},{4,5},{5,6},{6,7},{8,9},{9,10},{10,11},{12,13},{... | collective-permute-start | bytes 49160 | tf_op jit(solution)/shard_map/while/body/eval_jaxpr/ppermute | solution.py:18
  109.4 1.3 collective-permute-start.4
  110.7 4.3 %collective-permute-start.5 = (f32[2,8,1,256]{3,1,2,0:T(8,128)S(1)}, f32[2,8,1,256]{3,1,2,0:T(8,128)S(1)}, u32[]{:S(2)}, u32[]{:S(2)}) collective-permute-start(f32[2,8,1,256]{3,1,2,0:T(8,128)S(1)} %get-tuple-element.628), channel_id=1, source_target_pairs={{0,1},{1,2},{2,3},{4,5},{5,6},{6,7},{8,9},{9,10},{10,11},{12,13},{... | collective-permute-start | bytes 49160 | tf_op jit(solution)/shard_map/while/body/eval_jaxpr/ppermute | solution.py:18
  118.2 2.9 scatter_custom_fusion.17
  124.0 4.9 %collective-permute-start.7 = (f32[2,8,1,256]{3,1,2,0:T(8,128)S(1)}, f32[2,8,1,256]{3,1,2,0:T(8,128)S(1)}, u32[]{:S(2)}, u32[]{:S(2)}) collective-permute-start(f32[2,8,1,256]{3,1,2,0:T(8,128)S(1)} %get-tuple-element.646), channel_id=1, source_target_pairs={{0,1},{1,2},{2,3},{4,5},{5,6},{6,7},{8,9},{9,10},{10,11},{12,13},{... | collective-permute-start | bytes 49160 | tf_op jit(solution)/shard_map/while/body/eval_jaxpr/ppermute | solution.py:18
  131.6 1.3 collective-permute-start.8
  132.9 4.9 %collective-permute-start.9 = (f32[2,8,1,256]{3,1,2,0:T(8,128)S(1)}, f32[2,8,1,256]{3,1,2,0:T(8,128)S(1)}, u32[]{:S(2)}, u32[]{:S(2)}) collective-permute-start(f32[2,8,1,256]{3,1,2,0:T(8,128)S(1)} %get-tuple-element.662), channel_id=1, source_target_pairs={{0,1},{1,2},{2,3},{4,5},{5,6},{6,7},{8,9},{9,10},{10,11},{12,13},{... | collective-permute-start | bytes 49160 | tf_op jit(solution)/shard_map/while/body/eval_jaxpr/ppermute | solution.py:18
  141.7 4.9 %collective-permute-start.11 = (f32[2,8,1,256]{3,1,2,0:T(8,128)S(1)}, f32[2,8,1,256]{3,1,2,0:T(8,128)S(1)}, u32[]{:S(2)}, u32[]{:S(2)}) collective-permute-start(f32[2,8,1,256]{3,1,2,0:T(8,128)S(1)} %get-tuple-element.678), channel_id=1, source_target_pairs={{0,1},{1,2},{2,3},{4,5},{5,6},{6,7},{8,9},{9,10},{10,11},{12,13},{... | collective-permute-start | bytes 49160 | tf_op jit(solution)/shard_map/while/body/eval_jaxpr/ppermute | solution.py:18
  149.1 1.3 collective-permute-start.12
  150.4 11.2 %collective-permute-done.12 = f32[3,8,16,256]{3,1,2,0:T(8,128)S(1)} collective-permute-done((f32[3,8,16,256]{3,1,2,0:T(8,128)S(1)}, f32[3,8,16,256]{3,1,2,0:T(8,128)S(1)}, u32[]{:S(2)}, u32[]{:S(2)}) %collective-permute-start.12) | collective-permute-done | bytes 393248 | tf_op jit(solution)/shard_map/while/body/eval_jaxpr/ppermute | solution.py:27
  161.6 1.3 compare_select_fusion.5
  162.9 1.3 fusion.443
  164.8 2.8 scatter_custom_fusion.16
  170.1 4.4 %collective-permute-start.1 = (f32[2,8,1,256]{3,1,2,0:T(8,128)}, f32[2,8,1,256]{3,1,2,0:T(8,128)}, u32[]{:S(2)}, u32[]{:S(2)}) collective-permute-start(f32[2,8,1,256]{3,1,2,0:T(8,128)} %get-tuple-element.596), channel_id=1, source_target_pairs={{0,1},{1,2},{2,3},{4,5},{5,6},{6,7},{8,9},{9,10},{10,11},{12,13},{... | collective-permute-start | bytes 49160 | tf_op jit(solution)/shard_map/while/body/eval_jaxpr/ppermute | solution.py:18
  180.0 4.3 %collective-permute-start.3 = (f32[2,8,1,256]{3,1,2,0:T(8,128)S(1)}, f32[2,8,1,256]{3,1,2,0:T(8,128)S(1)}, u32[]{:S(2)}, u32[]{:S(2)}) collective-permute-start(f32[2,8,1,256]{3,1,2,0:T(8,128)S(1)} %get-tuple-element.612), channel_id=1, source_target_pairs={{0,1},{1,2},{2,3},{4,5},{5,6},{6,7},{8,9},{9,10},{10,11},{12,13},{... | collective-permute-start | bytes 49160 | tf_op jit(solution)/shard_map/while/body/eval_jaxpr/ppermute | solution.py:18
  188.2 4.3 %collective-permute-start.5 = (f32[2,8,1,256]{3,1,2,0:T(8,128)S(1)}, f32[2,8,1,256]{3,1,2,0:T(8,128)S(1)}, u32[]{:S(2)}, u32[]{:S(2)}) collective-permute-start(f32[2,8,1,256]{3,1,2,0:T(8,128)S(1)} %get-tuple-element.628), channel_id=1, source_target_pairs={{0,1},{1,2},{2,3},{4,5},{5,6},{6,7},{8,9},{9,10},{10,11},{12,13},{... | collective-permute-start | bytes 49160 | tf_op jit(solution)/shard_map/while/body/eval_jaxpr/ppermute | solution.py:18
  195.7 2.9 scatter_custom_fusion.17
  201.5 4.9 %collective-permute-start.7 = (f32[2,8,1,256]{3,1,2,0:T(8,128)S(1)}, f32[2,8,1,256]{3,1,2,0:T(8,128)S(1)}, u32[]{:S(2)}, u32[]{:S(2)}) collective-permute-start(f32[2,8,1,256]{3,1,2,0:T(8,128)S(1)} %get-tuple-element.646), channel_id=1, source_target_pairs={{0,1},{1,2},{2,3},{4,5},{5,6},{6,7},{8,9},{9,10},{10,11},{12,13},{... | collective-permute-start | bytes 49160 | tf_op jit(solution)/shard_map/while/body/eval_jaxpr/ppermute | solution.py:18
  210.4 4.9 %collective-permute-start.9 = (f32[2,8,1,256]{3,1,2,0:T(8,128)S(1)}, f32[2,8,1,256]{3,1,2,0:T(8,128)S(1)}, u32[]{:S(2)}, u32[]{:S(2)}) collective-permute-start(f32[2,8,1,256]{3,1,2,0:T(8,128)S(1)} %get-tuple-element.662), channel_id=1, source_target_pairs={{0,1},{1,2},{2,3},{4,5},{5,6},{6,7},{8,9},{9,10},{10,11},{12,13},{... | collective-permute-start | bytes 49160 | tf_op jit(solution)/shard_map/while/body/eval_jaxpr/ppermute | solution.py:18
  217.8 1.3 collective-permute-start.10
  219.1 4.9 %collective-permute-start.11 = (f32[2,8,1,256]{3,1,2,0:T(8,128)S(1)}, f32[2,8,1,256]{3,1,2,0:T(8,128)S(1)}, u32[]{:S(2)}, u32[]{:S(2)}) collective-permute-start(f32[2,8,1,256]{3,1,2,0:T(8,128)S(1)} %get-tuple-element.678), channel_id=1, source_target_pairs={{0,1},{1,2},{2,3},{4,5},{5,6},{6,7},{8,9},{9,10},{10,11},{12,13},{... | collective-permute-start | bytes 49160 | tf_op jit(solution)/shard_map/while/body/eval_jaxpr/ppermute | solution.py:18
  227.9 11.2 %collective-permute-done.12 = f32[3,8,16,256]{3,1,2,0:T(8,128)S(1)} collective-permute-done((f32[3,8,16,256]{3,1,2,0:T(8,128)S(1)}, f32[3,8,16,256]{3,1,2,0:T(8,128)S(1)}, u32[]{:S(2)}, u32[]{:S(2)}) %collective-permute-start.12) | collective-permute-done | bytes 393248 | tf_op jit(solution)/shard_map/while/body/eval_jaxpr/ppermute | solution.py:27
  239.7 3.1 scatter_custom_fusion.2
  243.5 3.1 collective-permute-start.13
  246.6 1.3 collective-permute-start.14
  249.2 2.4 collective-permute-done.14
  254.2 4.4 %collective-permute-start.15 = (f32[2,8,1,256]{3,1,2,0:T(8,128)S(1)}, f32[2,8,1,256]{3,1,2,0:T(8,128)S(1)}, u32[]{:S(2)}, u32[]{:S(2)}) collective-permute-start(f32[2,8,1,256]{3,1,2,0:T(8,128)S(1)} %get-tuple-element.376), channel_id=1, source_target_pairs={{0,1},{1,2},{2,3},{4,5},{5,6},{6,7},{8,9},{9,10},{10,11},{12,13},{... | collective-permute-start | bytes 49160 | tf_op jit(solution)/shard_map/ppermute | solution.py:18
  259.9 1.8 collective-permute-done.16
  263.4 3.9 %collective-permute-start.17 = (f32[2,8,1,256]{3,1,2,0:T(8,128)S(1)}, f32[2,8,1,256]{3,1,2,0:T(8,128)S(1)}, u32[]{:S(2)}, u32[]{:S(2)}) collective-permute-start(f32[2,8,1,256]{3,1,2,0:T(8,128)S(1)} %get-tuple-element.374), channel_id=1, source_target_pairs={{0,1},{1,2},{2,3},{4,5},{5,6},{6,7},{8,9},{9,10},{10,11},{12,13},{... | collective-permute-start | bytes 49160 | tf_op jit(solution)/shard_map/ppermute | solution.py:18
  267.3 1.3 collective-permute-start.18
  268.6 1.8 collective-permute-done.18
  273.5 2.9 scatter_custom_fusion.3
  277.7 3.9 %collective-permute-start.19 = (f32[2,8,1,256]{3,1,2,0:T(8,128)S(1)}, f32[2,8,1,256]{3,1,2,0:T(8,128)S(1)}, u32[]{:S(2)}, u32[]{:S(2)}) collective-permute-start(f32[2,8,1,256]{3,1,2,0:T(8,128)S(1)} %get-tuple-element.372), channel_id=1, source_target_pairs={{0,1},{1,2},{2,3},{4,5},{5,6},{6,7},{8,9},{9,10},{10,11},{12,13},{... | collective-permute-start | bytes 49160 | tf_op jit(solution)/shard_map/ppermute | solution.py:18
  281.6 1.3 collective-permute-start.20
  287.3 3.9 %collective-permute-start.21 = (f32[2,8,1,256]{3,1,2,0:T(8,128)S(1)}, f32[2,8,1,256]{3,1,2,0:T(8,128)S(1)}, u32[]{:S(2)}, u32[]{:S(2)}) collective-permute-start(f32[2,8,1,256]{3,1,2,0:T(8,128)S(1)} %get-tuple-element.370), channel_id=1, source_target_pairs={{0,1},{1,2},{2,3},{4,5},{5,6},{6,7},{8,9},{9,10},{10,11},{12,13},{... | collective-permute-start | bytes 49160 | tf_op jit(solution)/shard_map/ppermute | solution.py:18
  292.5 1.8 collective-permute-done.22
  296.0 3.9 %collective-permute-start.23 = (f32[2,8,1,256]{3,1,2,0:T(8,128)S(1)}, f32[2,8,1,256]{3,1,2,0:T(8,128)S(1)}, u32[]{:S(2)}, u32[]{:S(2)}) collective-permute-start(f32[2,8,1,256]{3,1,2,0:T(8,128)S(1)} %get-tuple-element.368), channel_id=1, source_target_pairs={{0,1},{1,2},{2,3},{4,5},{5,6},{6,7},{8,9},{9,10},{10,11},{12,13},{... | collective-permute-start | bytes 49160 | tf_op jit(solution)/shard_map/ppermute | solution.py:18
  301.2 1.8 collective-permute-done.24
  305.6 15.9 %all_gather.4 = f32[4,8,16,256]{3,2,1,0:T(8,128)S(1)} all-gather(f32[1,8,16,256]{3,2,1,0:T(8,128)S(1)} %copy.228), channel_id=1, replica_groups=mesh['groups'=2,'win'=4,'lat'=4] {'win'}, dimensions={0}, use_global_device_ids=true | all-gather | bytes 655360 | tf_op jit(solution)/shard_map/all_gather | solution.py:97
  (576 shorter events, 102.9 us)
Async XLA Ops:
  3.7 3.3 %copy-start.18 = (f32[8,8]{0,1:T(8,128)}, f32[8,8]{0,1:T(8,128)S(1)}, u32[]{:S(2)}) copy-start(f32[8,8]{0,1:T(8,128)S(1)} %copy.184) | copy-start | bytes 772
  7.0 24.8 %copy-start = (f32[1,2,3,8,16,256]{5,3,4,2,1,0:T(8,128)}, f32[1,2,3,8,16,256]{5,3,4,2,1,0:T(8,128)S(1)}, u32[]{:S(2)}) copy-start(f32[1,2,3,8,16,256]{5,3,4,2,1,0:T(8,128)S(1)} %get-tuple-element.716) | copy-start | bytes 2359300 | tf_op jit(solution)/shard_map/while
  14.3 6.6 %collective-permute-start = (f32[2,8,1,256]{3,1,2,0:T(8,128)}, f32[2,8,1,256]{3,1,2,0:T(8,128)}, u32[]{:S(2)}, u32[]{:S(2)}) collective-permute-start(f32[2,8,1,256]{3,1,2,0:T(8,128)} %get-tuple-element.595), channel_id=1, source_target_pairs={{1,0},{2,1},{3,2},{5,4},{6,5},{7,6},{9,8},{10,9},{11,10},{13,12},{... | collective-permute-start | bytes 49160 | tf_op jit(solution)/shard_map/while/body/eval_jaxpr/ppermute | solution.py:19
  15.6 5.4 %collective-permute-start.1 = (f32[2,8,1,256]{3,1,2,0:T(8,128)}, f32[2,8,1,256]{3,1,2,0:T(8,128)}, u32[]{:S(2)}, u32[]{:S(2)}) collective-permute-start(f32[2,8,1,256]{3,1,2,0:T(8,128)} %get-tuple-element.596), channel_id=1, source_target_pairs={{0,1},{1,2},{2,3},{4,5},{5,6},{6,7},{8,9},{9,10},{10,11},{12,13},{... | collective-permute-start | bytes 49160 | tf_op jit(solution)/shard_map/while/body/eval_jaxpr/ppermute | solution.py:18
  23.5 5.8 %collective-permute-start.2 = (f32[2,8,1,256]{3,1,2,0:T(8,128)S(1)}, f32[2,8,1,256]{3,1,2,0:T(8,128)S(1)}, u32[]{:S(2)}, u32[]{:S(2)}) collective-permute-start(f32[2,8,1,256]{3,1,2,0:T(8,128)S(1)} %get-tuple-element.611), channel_id=1, source_target_pairs={{1,0},{2,1},{3,2},{5,4},{6,5},{7,6},{9,8},{10,9},{11,10},{13,12},{... | collective-permute-start | bytes 49160 | tf_op jit(solution)/shard_map/while/body/eval_jaxpr/ppermute | solution.py:19
  24.8 5.4 %collective-permute-start.3 = (f32[2,8,1,256]{3,1,2,0:T(8,128)S(1)}, f32[2,8,1,256]{3,1,2,0:T(8,128)S(1)}, u32[]{:S(2)}, u32[]{:S(2)}) collective-permute-start(f32[2,8,1,256]{3,1,2,0:T(8,128)S(1)} %get-tuple-element.612), channel_id=1, source_target_pairs={{0,1},{1,2},{2,3},{4,5},{5,6},{6,7},{8,9},{9,10},{10,11},{12,13},{... | collective-permute-start | bytes 49160 | tf_op jit(solution)/shard_map/while/body/eval_jaxpr/ppermute | solution.py:18
  31.9 5.6 %collective-permute-start.4 = (f32[2,8,1,256]{3,1,2,0:T(8,128)S(1)}, f32[2,8,1,256]{3,1,2,0:T(8,128)S(1)}, u32[]{:S(2)}, u32[]{:S(2)}) collective-permute-start(f32[2,8,1,256]{3,1,2,0:T(8,128)S(1)} %get-tuple-element.627), channel_id=1, source_target_pairs={{1,0},{2,1},{3,2},{5,4},{6,5},{7,6},{9,8},{10,9},{11,10},{13,12},{... | collective-permute-start | bytes 49160 | tf_op jit(solution)/shard_map/while/body/eval_jaxpr/ppermute | solution.py:19
  33.2 5.1 %collective-permute-start.5 = (f32[2,8,1,256]{3,1,2,0:T(8,128)S(1)}, f32[2,8,1,256]{3,1,2,0:T(8,128)S(1)}, u32[]{:S(2)}, u32[]{:S(2)}) collective-permute-start(f32[2,8,1,256]{3,1,2,0:T(8,128)S(1)} %get-tuple-element.628), channel_id=1, source_target_pairs={{0,1},{1,2},{2,3},{4,5},{5,6},{6,7},{8,9},{9,10},{10,11},{12,13},{... | collective-permute-start | bytes 49160 | tf_op jit(solution)/shard_map/while/body/eval_jaxpr/ppermute | solution.py:18
  45.2 6.8 %collective-permute-start.6 = (f32[2,8,1,256]{3,1,2,0:T(8,128)S(1)}, f32[2,8,1,256]{3,1,2,0:T(8,128)S(1)}, u32[]{:S(2)}, u32[]{:S(2)}) collective-permute-start(f32[2,8,1,256]{3,1,2,0:T(8,128)S(1)} %get-tuple-element.645), channel_id=1, source_target_pairs={{1,0},{2,1},{3,2},{5,4},{6,5},{7,6},{9,8},{10,9},{11,10},{13,12},{... | collective-permute-start | bytes 49160 | tf_op jit(solution)/shard_map/while/body/eval_jaxpr/ppermute | solution.py:19
  46.5 5.7 %collective-permute-start.7 = (f32[2,8,1,256]{3,1,2,0:T(8,128)S(1)}, f32[2,8,1,256]{3,1,2,0:T(8,128)S(1)}, u32[]{:S(2)}, u32[]{:S(2)}) collective-permute-start(f32[2,8,1,256]{3,1,2,0:T(8,128)S(1)} %get-tuple-element.646), channel_id=1, source_target_pairs={{0,1},{1,2},{2,3},{4,5},{5,6},{6,7},{8,9},{9,10},{10,11},{12,13},{... | collective-permute-start | bytes 49160 | tf_op jit(solution)/shard_map/while/body/eval_jaxpr/ppermute | solution.py:18
  51.4 1.6 copy-start.9
  51.4 1.6 copy-start.13
  54.1 6.2 %collective-permute-start.8 = (f32[2,8,1,256]{3,1,2,0:T(8,128)S(1)}, f32[2,8,1,256]{3,1,2,0:T(8,128)S(1)}, u32[]{:S(2)}, u32[]{:S(2)}) collective-permute-start(f32[2,8,1,256]{3,1,2,0:T(8,128)S(1)} %get-tuple-element.661), channel_id=1, source_target_pairs={{1,0},{2,1},{3,2},{5,4},{6,5},{7,6},{9,8},{10,9},{11,10},{13,12},{... | collective-permute-start | bytes 49160 | tf_op jit(solution)/shard_map/while/body/eval_jaxpr/ppermute | solution.py:19
  55.4 5.7 %collective-permute-start.9 = (f32[2,8,1,256]{3,1,2,0:T(8,128)S(1)}, f32[2,8,1,256]{3,1,2,0:T(8,128)S(1)}, u32[]{:S(2)}, u32[]{:S(2)}) collective-permute-start(f32[2,8,1,256]{3,1,2,0:T(8,128)S(1)} %get-tuple-element.662), channel_id=1, source_target_pairs={{0,1},{1,2},{2,3},{4,5},{5,6},{6,7},{8,9},{9,10},{10,11},{12,13},{... | collective-permute-start | bytes 49160 | tf_op jit(solution)/shard_map/while/body/eval_jaxpr/ppermute | solution.py:18
  62.9 6.2 %collective-permute-start.10 = (f32[2,8,1,256]{3,1,2,0:T(8,128)S(1)}, f32[2,8,1,256]{3,1,2,0:T(8,128)S(1)}, u32[]{:S(2)}, u32[]{:S(2)}) collective-permute-start(f32[2,8,1,256]{3,1,2,0:T(8,128)S(1)} %get-tuple-element.677), channel_id=1, source_target_pairs={{1,0},{2,1},{3,2},{5,4},{6,5},{7,6},{9,8},{10,9},{11,10},{13,12},{... | collective-permute-start | bytes 49160 | tf_op jit(solution)/shard_map/while/body/eval_jaxpr/ppermute | solution.py:19
  64.2 5.7 %collective-permute-start.11 = (f32[2,8,1,256]{3,1,2,0:T(8,128)S(1)}, f32[2,8,1,256]{3,1,2,0:T(8,128)S(1)}, u32[]{:S(2)}, u32[]{:S(2)}) collective-permute-start(f32[2,8,1,256]{3,1,2,0:T(8,128)S(1)} %get-tuple-element.678), channel_id=1, source_target_pairs={{0,1},{1,2},{2,3},{4,5},{5,6},{6,7},{8,9},{9,10},{10,11},{12,13},{... | collective-permute-start | bytes 49160 | tf_op jit(solution)/shard_map/while/body/eval_jaxpr/ppermute | solution.py:18
  71.6 12.5 %collective-permute-start.12 = (f32[3,8,16,256]{3,1,2,0:T(8,128)S(1)}, f32[3,8,16,256]{3,1,2,0:T(8,128)S(1)}, u32[]{:S(2)}, u32[]{:S(2)}) collective-permute-start(f32[3,8,16,256]{3,1,2,0:T(8,128)S(1)} %fusion.479), channel_id=1, source_target_pairs={{4,0},{8,4},{12,8},{5,1},{9,5},{13,9},{6,2},{10,6},{14,10},{7,3},{... | collective-permute-start | bytes 1179656 | tf_op jit(solution)/shard_map/while/body/eval_jaxpr/ppermute | solution.py:27
  84.1 25.3 %copy-start = (f32[1,2,3,8,16,256]{5,3,4,2,1,0:T(8,128)}, f32[1,2,3,8,16,256]{5,3,4,2,1,0:T(8,128)S(1)}, u32[]{:S(2)}) copy-start(f32[1,2,3,8,16,256]{5,3,4,2,1,0:T(8,128)S(1)} %get-tuple-element.716) | copy-start | bytes 2359300 | tf_op jit(solution)/shard_map/while
  91.3 7.4 %collective-permute-start = (f32[2,8,1,256]{3,1,2,0:T(8,128)}, f32[2,8,1,256]{3,1,2,0:T(8,128)}, u32[]{:S(2)}, u32[]{:S(2)}) collective-permute-start(f32[2,8,1,256]{3,1,2,0:T(8,128)} %get-tuple-element.595), channel_id=1, source_target_pairs={{1,0},{2,1},{3,2},{5,4},{6,5},{7,6},{9,8},{10,9},{11,10},{13,12},{... | collective-permute-start | bytes 49160 | tf_op jit(solution)/shard_map/while/body/eval_jaxpr/ppermute | solution.py:19
  92.6 6.1 %collective-permute-start.1 = (f32[2,8,1,256]{3,1,2,0:T(8,128)}, f32[2,8,1,256]{3,1,2,0:T(8,128)}, u32[]{:S(2)}, u32[]{:S(2)}) collective-permute-start(f32[2,8,1,256]{3,1,2,0:T(8,128)} %get-tuple-element.596), channel_id=1, source_target_pairs={{0,1},{1,2},{2,3},{4,5},{5,6},{6,7},{8,9},{9,10},{10,11},{12,13},{... | collective-permute-start | bytes 49160 | tf_op jit(solution)/shard_map/while/body/eval_jaxpr/ppermute | solution.py:18
  101.2 5.6 %collective-permute-start.2 = (f32[2,8,1,256]{3,1,2,0:T(8,128)S(1)}, f32[2,8,1,256]{3,1,2,0:T(8,128)S(1)}, u32[]{:S(2)}, u32[]{:S(2)}) collective-permute-start(f32[2,8,1,256]{3,1,2,0:T(8,128)S(1)} %get-tuple-element.611), channel_id=1, source_target_pairs={{1,0},{2,1},{3,2},{5,4},{6,5},{7,6},{9,8},{10,9},{11,10},{13,12},{... | collective-permute-start | bytes 49160 | tf_op jit(solution)/shard_map/while/body/eval_jaxpr/ppermute | solution.py:19
  102.5 5.1 %collective-permute-start.3 = (f32[2,8,1,256]{3,1,2,0:T(8,128)S(1)}, f32[2,8,1,256]{3,1,2,0:T(8,128)S(1)}, u32[]{:S(2)}, u32[]{:S(2)}) collective-permute-start(f32[2,8,1,256]{3,1,2,0:T(8,128)S(1)} %get-tuple-element.612), channel_id=1, source_target_pairs={{0,1},{1,2},{2,3},{4,5},{5,6},{6,7},{8,9},{9,10},{10,11},{12,13},{... | collective-permute-start | bytes 49160 | tf_op jit(solution)/shard_map/while/body/eval_jaxpr/ppermute | solution.py:18
  109.4 5.6 %collective-permute-start.4 = (f32[2,8,1,256]{3,1,2,0:T(8,128)S(1)}, f32[2,8,1,256]{3,1,2,0:T(8,128)S(1)}, u32[]{:S(2)}, u32[]{:S(2)}) collective-permute-start(f32[2,8,1,256]{3,1,2,0:T(8,128)S(1)} %get-tuple-element.627), channel_id=1, source_target_pairs={{1,0},{2,1},{3,2},{5,4},{6,5},{7,6},{9,8},{10,9},{11,10},{13,12},{... | collective-permute-start | bytes 49160 | tf_op jit(solution)/shard_map/while/body/eval_jaxpr/ppermute | solution.py:19
  110.7 5.1 %collective-permute-start.5 = (f32[2,8,1,256]{3,1,2,0:T(8,128)S(1)}, f32[2,8,1,256]{3,1,2,0:T(8,128)S(1)}, u32[]{:S(2)}, u32[]{:S(2)}) collective-permute-start(f32[2,8,1,256]{3,1,2,0:T(8,128)S(1)} %get-tuple-element.628), channel_id=1, source_target_pairs={{0,1},{1,2},{2,3},{4,5},{5,6},{6,7},{8,9},{9,10},{10,11},{12,13},{... | collective-permute-start | bytes 49160 | tf_op jit(solution)/shard_map/while/body/eval_jaxpr/ppermute | solution.py:18
  122.7 6.8 %collective-permute-start.6 = (f32[2,8,1,256]{3,1,2,0:T(8,128)S(1)}, f32[2,8,1,256]{3,1,2,0:T(8,128)S(1)}, u32[]{:S(2)}, u32[]{:S(2)}) collective-permute-start(f32[2,8,1,256]{3,1,2,0:T(8,128)S(1)} %get-tuple-element.645), channel_id=1, source_target_pairs={{1,0},{2,1},{3,2},{5,4},{6,5},{7,6},{9,8},{10,9},{11,10},{13,12},{... | collective-permute-start | bytes 49160 | tf_op jit(solution)/shard_map/while/body/eval_jaxpr/ppermute | solution.py:19
  124.0 5.7 %collective-permute-start.7 = (f32[2,8,1,256]{3,1,2,0:T(8,128)S(1)}, f32[2,8,1,256]{3,1,2,0:T(8,128)S(1)}, u32[]{:S(2)}, u32[]{:S(2)}) collective-permute-start(f32[2,8,1,256]{3,1,2,0:T(8,128)S(1)} %get-tuple-element.646), channel_id=1, source_target_pairs={{0,1},{1,2},{2,3},{4,5},{5,6},{6,7},{8,9},{9,10},{10,11},{12,13},{... | collective-permute-start | bytes 49160 | tf_op jit(solution)/shard_map/while/body/eval_jaxpr/ppermute | solution.py:18
  128.8 1.6 copy-start.9
  128.9 1.6 copy-start.13
  131.6 6.2 %collective-permute-start.8 = (f32[2,8,1,256]{3,1,2,0:T(8,128)S(1)}, f32[2,8,1,256]{3,1,2,0:T(8,128)S(1)}, u32[]{:S(2)}, u32[]{:S(2)}) collective-permute-start(f32[2,8,1,256]{3,1,2,0:T(8,128)S(1)} %get-tuple-element.661), channel_id=1, source_target_pairs={{1,0},{2,1},{3,2},{5,4},{6,5},{7,6},{9,8},{10,9},{11,10},{13,12},{... | collective-permute-start | bytes 49160 | tf_op jit(solution)/shard_map/while/body/eval_jaxpr/ppermute | solution.py:19
  132.9 5.7 %collective-permute-start.9 = (f32[2,8,1,256]{3,1,2,0:T(8,128)S(1)}, f32[2,8,1,256]{3,1,2,0:T(8,128)S(1)}, u32[]{:S(2)}, u32[]{:S(2)}) collective-permute-start(f32[2,8,1,256]{3,1,2,0:T(8,128)S(1)} %get-tuple-element.662), channel_id=1, source_target_pairs={{0,1},{1,2},{2,3},{4,5},{5,6},{6,7},{8,9},{9,10},{10,11},{12,13},{... | collective-permute-start | bytes 49160 | tf_op jit(solution)/shard_map/while/body/eval_jaxpr/ppermute | solution.py:18
  140.3 6.2 %collective-permute-start.10 = (f32[2,8,1,256]{3,1,2,0:T(8,128)S(1)}, f32[2,8,1,256]{3,1,2,0:T(8,128)S(1)}, u32[]{:S(2)}, u32[]{:S(2)}) collective-permute-start(f32[2,8,1,256]{3,1,2,0:T(8,128)S(1)} %get-tuple-element.677), channel_id=1, source_target_pairs={{1,0},{2,1},{3,2},{5,4},{6,5},{7,6},{9,8},{10,9},{11,10},{13,12},{... | collective-permute-start | bytes 49160 | tf_op jit(solution)/shard_map/while/body/eval_jaxpr/ppermute | solution.py:19
  141.7 5.7 %collective-permute-start.11 = (f32[2,8,1,256]{3,1,2,0:T(8,128)S(1)}, f32[2,8,1,256]{3,1,2,0:T(8,128)S(1)}, u32[]{:S(2)}, u32[]{:S(2)}) collective-permute-start(f32[2,8,1,256]{3,1,2,0:T(8,128)S(1)} %get-tuple-element.678), channel_id=1, source_target_pairs={{0,1},{1,2},{2,3},{4,5},{5,6},{6,7},{8,9},{9,10},{10,11},{12,13},{... | collective-permute-start | bytes 49160 | tf_op jit(solution)/shard_map/while/body/eval_jaxpr/ppermute | solution.py:18
  149.1 12.5 %collective-permute-start.12 = (f32[3,8,16,256]{3,1,2,0:T(8,128)S(1)}, f32[3,8,16,256]{3,1,2,0:T(8,128)S(1)}, u32[]{:S(2)}, u32[]{:S(2)}) collective-permute-start(f32[3,8,16,256]{3,1,2,0:T(8,128)S(1)} %fusion.479), channel_id=1, source_target_pairs={{4,0},{8,4},{12,8},{5,1},{9,5},{13,9},{6,2},{10,6},{14,10},{7,3},{... | collective-permute-start | bytes 1179656 | tf_op jit(solution)/shard_map/while/body/eval_jaxpr/ppermute | solution.py:27
  161.6 25.3 %copy-start = (f32[1,2,3,8,16,256]{5,3,4,2,1,0:T(8,128)}, f32[1,2,3,8,16,256]{5,3,4,2,1,0:T(8,128)S(1)}, u32[]{:S(2)}) copy-start(f32[1,2,3,8,16,256]{5,3,4,2,1,0:T(8,128)S(1)} %get-tuple-element.716) | copy-start | bytes 2359300 | tf_op jit(solution)/shard_map/while
  168.8 7.4 %collective-permute-start = (f32[2,8,1,256]{3,1,2,0:T(8,128)}, f32[2,8,1,256]{3,1,2,0:T(8,128)}, u32[]{:S(2)}, u32[]{:S(2)}) collective-permute-start(f32[2,8,1,256]{3,1,2,0:T(8,128)} %get-tuple-element.595), channel_id=1, source_target_pairs={{1,0},{2,1},{3,2},{5,4},{6,5},{7,6},{9,8},{10,9},{11,10},{13,12},{... | collective-permute-start | bytes 49160 | tf_op jit(solution)/shard_map/while/body/eval_jaxpr/ppermute | solution.py:19
  170.1 6.1 %collective-permute-start.1 = (f32[2,8,1,256]{3,1,2,0:T(8,128)}, f32[2,8,1,256]{3,1,2,0:T(8,128)}, u32[]{:S(2)}, u32[]{:S(2)}) collective-permute-start(f32[2,8,1,256]{3,1,2,0:T(8,128)} %get-tuple-element.596), channel_id=1, source_target_pairs={{0,1},{1,2},{2,3},{4,5},{5,6},{6,7},{8,9},{9,10},{10,11},{12,13},{... | collective-permute-start | bytes 49160 | tf_op jit(solution)/shard_map/while/body/eval_jaxpr/ppermute | solution.py:18
  178.7 5.6 %collective-permute-start.2 = (f32[2,8,1,256]{3,1,2,0:T(8,128)S(1)}, f32[2,8,1,256]{3,1,2,0:T(8,128)S(1)}, u32[]{:S(2)}, u32[]{:S(2)}) collective-permute-start(f32[2,8,1,256]{3,1,2,0:T(8,128)S(1)} %get-tuple-element.611), channel_id=1, source_target_pairs={{1,0},{2,1},{3,2},{5,4},{6,5},{7,6},{9,8},{10,9},{11,10},{13,12},{... | collective-permute-start | bytes 49160 | tf_op jit(solution)/shard_map/while/body/eval_jaxpr/ppermute | solution.py:19
  180.0 5.1 %collective-permute-start.3 = (f32[2,8,1,256]{3,1,2,0:T(8,128)S(1)}, f32[2,8,1,256]{3,1,2,0:T(8,128)S(1)}, u32[]{:S(2)}, u32[]{:S(2)}) collective-permute-start(f32[2,8,1,256]{3,1,2,0:T(8,128)S(1)} %get-tuple-element.612), channel_id=1, source_target_pairs={{0,1},{1,2},{2,3},{4,5},{5,6},{6,7},{8,9},{9,10},{10,11},{12,13},{... | collective-permute-start | bytes 49160 | tf_op jit(solution)/shard_map/while/body/eval_jaxpr/ppermute | solution.py:18
  186.9 5.6 %collective-permute-start.4 = (f32[2,8,1,256]{3,1,2,0:T(8,128)S(1)}, f32[2,8,1,256]{3,1,2,0:T(8,128)S(1)}, u32[]{:S(2)}, u32[]{:S(2)}) collective-permute-start(f32[2,8,1,256]{3,1,2,0:T(8,128)S(1)} %get-tuple-element.627), channel_id=1, source_target_pairs={{1,0},{2,1},{3,2},{5,4},{6,5},{7,6},{9,8},{10,9},{11,10},{13,12},{... | collective-permute-start | bytes 49160 | tf_op jit(solution)/shard_map/while/body/eval_jaxpr/ppermute | solution.py:19
  188.2 5.1 %collective-permute-start.5 = (f32[2,8,1,256]{3,1,2,0:T(8,128)S(1)}, f32[2,8,1,256]{3,1,2,0:T(8,128)S(1)}, u32[]{:S(2)}, u32[]{:S(2)}) collective-permute-start(f32[2,8,1,256]{3,1,2,0:T(8,128)S(1)} %get-tuple-element.628), channel_id=1, source_target_pairs={{0,1},{1,2},{2,3},{4,5},{5,6},{6,7},{8,9},{9,10},{10,11},{12,13},{... | collective-permute-start | bytes 49160 | tf_op jit(solution)/shard_map/while/body/eval_jaxpr/ppermute | solution.py:18
  200.2 6.8 %collective-permute-start.6 = (f32[2,8,1,256]{3,1,2,0:T(8,128)S(1)}, f32[2,8,1,256]{3,1,2,0:T(8,128)S(1)}, u32[]{:S(2)}, u32[]{:S(2)}) collective-permute-start(f32[2,8,1,256]{3,1,2,0:T(8,128)S(1)} %get-tuple-element.645), channel_id=1, source_target_pairs={{1,0},{2,1},{3,2},{5,4},{6,5},{7,6},{9,8},{10,9},{11,10},{13,12},{... | collective-permute-start | bytes 49160 | tf_op jit(solution)/shard_map/while/body/eval_jaxpr/ppermute | solution.py:19
  201.5 5.7 %collective-permute-start.7 = (f32[2,8,1,256]{3,1,2,0:T(8,128)S(1)}, f32[2,8,1,256]{3,1,2,0:T(8,128)S(1)}, u32[]{:S(2)}, u32[]{:S(2)}) collective-permute-start(f32[2,8,1,256]{3,1,2,0:T(8,128)S(1)} %get-tuple-element.646), channel_id=1, source_target_pairs={{0,1},{1,2},{2,3},{4,5},{5,6},{6,7},{8,9},{9,10},{10,11},{12,13},{... | collective-permute-start | bytes 49160 | tf_op jit(solution)/shard_map/while/body/eval_jaxpr/ppermute | solution.py:18
  206.3 1.6 copy-start.9
  209.1 6.2 %collective-permute-start.8 = (f32[2,8,1,256]{3,1,2,0:T(8,128)S(1)}, f32[2,8,1,256]{3,1,2,0:T(8,128)S(1)}, u32[]{:S(2)}, u32[]{:S(2)}) collective-permute-start(f32[2,8,1,256]{3,1,2,0:T(8,128)S(1)} %get-tuple-element.661), channel_id=1, source_target_pairs={{1,0},{2,1},{3,2},{5,4},{6,5},{7,6},{9,8},{10,9},{11,10},{13,12},{... | collective-permute-start | bytes 49160 | tf_op jit(solution)/shard_map/while/body/eval_jaxpr/ppermute | solution.py:19
  210.4 5.7 %collective-permute-start.9 = (f32[2,8,1,256]{3,1,2,0:T(8,128)S(1)}, f32[2,8,1,256]{3,1,2,0:T(8,128)S(1)}, u32[]{:S(2)}, u32[]{:S(2)}) collective-permute-start(f32[2,8,1,256]{3,1,2,0:T(8,128)S(1)} %get-tuple-element.662), channel_id=1, source_target_pairs={{0,1},{1,2},{2,3},{4,5},{5,6},{6,7},{8,9},{9,10},{10,11},{12,13},{... | collective-permute-start | bytes 49160 | tf_op jit(solution)/shard_map/while/body/eval_jaxpr/ppermute | solution.py:18
  217.8 6.2 %collective-permute-start.10 = (f32[2,8,1,256]{3,1,2,0:T(8,128)S(1)}, f32[2,8,1,256]{3,1,2,0:T(8,128)S(1)}, u32[]{:S(2)}, u32[]{:S(2)}) collective-permute-start(f32[2,8,1,256]{3,1,2,0:T(8,128)S(1)} %get-tuple-element.677), channel_id=1, source_target_pairs={{1,0},{2,1},{3,2},{5,4},{6,5},{7,6},{9,8},{10,9},{11,10},{13,12},{... | collective-permute-start | bytes 49160 | tf_op jit(solution)/shard_map/while/body/eval_jaxpr/ppermute | solution.py:19
  219.1 5.7 %collective-permute-start.11 = (f32[2,8,1,256]{3,1,2,0:T(8,128)S(1)}, f32[2,8,1,256]{3,1,2,0:T(8,128)S(1)}, u32[]{:S(2)}, u32[]{:S(2)}) collective-permute-start(f32[2,8,1,256]{3,1,2,0:T(8,128)S(1)} %get-tuple-element.678), channel_id=1, source_target_pairs={{0,1},{1,2},{2,3},{4,5},{5,6},{6,7},{8,9},{9,10},{10,11},{12,13},{... | collective-permute-start | bytes 49160 | tf_op jit(solution)/shard_map/while/body/eval_jaxpr/ppermute | solution.py:18
  226.6 12.5 %collective-permute-start.12 = (f32[3,8,16,256]{3,1,2,0:T(8,128)S(1)}, f32[3,8,16,256]{3,1,2,0:T(8,128)S(1)}, u32[]{:S(2)}, u32[]{:S(2)}) collective-permute-start(f32[3,8,16,256]{3,1,2,0:T(8,128)S(1)} %fusion.479), channel_id=1, source_target_pairs={{4,0},{8,4},{12,8},{5,1},{9,5},{13,9},{6,2},{10,6},{14,10},{7,3},{... | collective-permute-start | bytes 1179656 | tf_op jit(solution)/shard_map/while/body/eval_jaxpr/ppermute | solution.py:27
  243.4 4.5 %copy-start.14 = (f32[1,8,16,256]{3,1,2,0:T(8,128)}, f32[1,8,16,256]{3,1,2,0:T(8,128)S(1)}, u32[]{:S(2)}) copy-start(f32[1,8,16,256]{3,1,2,0:T(8,128)S(1)} %get-tuple-element.430) | copy-start | bytes 393220
  243.5 5.7 %collective-permute-start.13 = (f32[2,8,1,256]{3,1,2,0:T(8,128)S(1)}, f32[2,8,1,256]{3,1,2,0:T(8,128)S(1)}, u32[]{:S(2)}, u32[]{:S(2)}) collective-permute-start(f32[2,8,1,256]{3,1,2,0:T(8,128)S(1)} %get-tuple-element.378), channel_id=1, source_target_pairs={{0,1},{1,2},{2,3},{4,5},{5,6},{6,7},{8,9},{9,10},{10,11},{12,13},{... | collective-permute-start | bytes 49160 | tf_op jit(solution)/shard_map/ppermute | solution.py:18
  246.6 4.9 %collective-permute-start.14 = (f32[2,8,1,256]{3,1,2,0:T(8,128)S(1)}, f32[2,8,1,256]{3,1,2,0:T(8,128)S(1)}, u32[]{:S(2)}, u32[]{:S(2)}) collective-permute-start(f32[2,8,1,256]{3,1,2,0:T(8,128)S(1)} %get-tuple-element.379), channel_id=1, source_target_pairs={{1,0},{2,1},{3,2},{5,4},{6,5},{7,6},{9,8},{10,9},{11,10},{13,12},{... | collective-permute-start | bytes 49160 | tf_op jit(solution)/shard_map/ppermute | solution.py:19
  247.9 5.3 %copy-start.10 = (f32[8,1,1]{0,2,1:T(1,128)S(1)}, f32[8,1,1]{0,2,1:T(1,128)}, u32[]{:S(2)}) copy-start(f32[8,1,1]{0,2,1:T(1,128)} %get-tuple-element.725) | copy-start | bytes 100
  254.2 5.7 %collective-permute-start.15 = (f32[2,8,1,256]{3,1,2,0:T(8,128)S(1)}, f32[2,8,1,256]{3,1,2,0:T(8,128)S(1)}, u32[]{:S(2)}, u32[]{:S(2)}) collective-permute-start(f32[2,8,1,256]{3,1,2,0:T(8,128)S(1)} %get-tuple-element.376), channel_id=1, source_target_pairs={{0,1},{1,2},{2,3},{4,5},{5,6},{6,7},{8,9},{9,10},{10,11},{12,13},{... | collective-permute-start | bytes 49160 | tf_op jit(solution)/shard_map/ppermute | solution.py:18
  258.6 3.1 collective-permute-start.16
  263.4 5.2 %collective-permute-start.17 = (f32[2,8,1,256]{3,1,2,0:T(8,128)S(1)}, f32[2,8,1,256]{3,1,2,0:T(8,128)S(1)}, u32[]{:S(2)}, u32[]{:S(2)}) collective-permute-start(f32[2,8,1,256]{3,1,2,0:T(8,128)S(1)} %get-tuple-element.374), channel_id=1, source_target_pairs={{0,1},{1,2},{2,3},{4,5},{5,6},{6,7},{8,9},{9,10},{10,11},{12,13},{... | collective-permute-start | bytes 49160 | tf_op jit(solution)/shard_map/ppermute | solution.py:18
  267.3 3.1 collective-permute-start.18
  273.5 3.5 %copy-start.6 = (f32[3,8,16,256]{3,1,2,0:T(8,128)S(1)}, f32[3,8,16,256]{3,1,2,0:T(8,128)}, u32[]{:S(2)}) copy-start(f32[3,8,16,256]{3,1,2,0:T(8,128)} %copy-done.2) | copy-start | bytes 1179652
  277.0 18.8 %copy-start.4 = (f32[3,8,16,256]{3,1,2,0:T(8,128)}, f32[3,8,16,256]{3,1,2,0:T(8,128)S(1)}, u32[]{:S(2)}) copy-start(f32[3,8,16,256]{3,1,2,0:T(8,128)S(1)} %get-tuple-element.417) | copy-start | bytes 1179652
  277.7 6.4 %collective-permute-start.19 = (f32[2,8,1,256]{3,1,2,0:T(8,128)S(1)}, f32[2,8,1,256]{3,1,2,0:T(8,128)S(1)}, u32[]{:S(2)}, u32[]{:S(2)}) collective-permute-start(f32[2,8,1,256]{3,1,2,0:T(8,128)S(1)} %get-tuple-element.372), channel_id=1, source_target_pairs={{0,1},{1,2},{2,3},{4,5},{5,6},{6,7},{8,9},{9,10},{10,11},{12,13},{... | collective-permute-start | bytes 49160 | tf_op jit(solution)/shard_map/ppermute | solution.py:18
  281.6 3.1 collective-permute-start.20
  287.3 5.2 %collective-permute-start.21 = (f32[2,8,1,256]{3,1,2,0:T(8,128)S(1)}, f32[2,8,1,256]{3,1,2,0:T(8,128)S(1)}, u32[]{:S(2)}, u32[]{:S(2)}) collective-permute-start(f32[2,8,1,256]{3,1,2,0:T(8,128)S(1)} %get-tuple-element.370), channel_id=1, source_target_pairs={{0,1},{1,2},{2,3},{4,5},{5,6},{6,7},{8,9},{9,10},{10,11},{12,13},{... | collective-permute-start | bytes 49160 | tf_op jit(solution)/shard_map/ppermute | solution.py:18
  291.2 3.1 collective-permute-start.22
  296.0 5.2 %collective-permute-start.23 = (f32[2,8,1,256]{3,1,2,0:T(8,128)S(1)}, f32[2,8,1,256]{3,1,2,0:T(8,128)S(1)}, u32[]{:S(2)}, u32[]{:S(2)}) collective-permute-start(f32[2,8,1,256]{3,1,2,0:T(8,128)S(1)} %get-tuple-element.368), channel_id=1, source_target_pairs={{0,1},{1,2},{2,3},{4,5},{5,6},{6,7},{8,9},{9,10},{10,11},{12,13},{... | collective-permute-start | bytes 49160 | tf_op jit(solution)/shard_map/ppermute | solution.py:18
  299.9 3.1 collective-permute-start.24
  (28 other events, 33.8 us)
